TPU v7x, 256 devices: a whole 4x4x8 slice. The times are simulated.
256 devices in a mesh: sub: 128 (over x, y, z_hi, core), panel: 2 (over z_lo).
Axes of the slice: x: 4, y: 4, z: 8 (z_hi: 4, z_lo: 2; z = z_hi * 2 + z_lo), core: 2. Of those that a mesh axis runs over, the one named last changes fastest.
Arguments:
- solution: float32 [131072, 256], P('sub', 'panel'), may hold values from -6 to 6
- residual: float32 [131072, 256], P('sub', 'panel'), may hold values from -25 to 25
- shadow: float32 [131072, 256], P('sub', 'panel'), may hold values from -120 to 120
- direction: float32 [131072, 256], P('sub', 'panel'), may hold values from -6 to 6
- old_image: float32 [131072, 256], P('sub', 'panel'), may hold values from -6 to 6
- rho_prev: float32 [256], P('panel'), may hold values from 1 to 4
- alpha_prev: float32 [256], P('panel'), may hold values from 0.5 to 2
- omega_prev: float32 [256], P('panel'), may hold values from 0.5 to 2
- lower_inverse: bfloat16 [128, 1792, 1792], P('sub', None, 'panel'), may hold values from -0.4 to 0.4, as said below
- upper_inverse: bfloat16 [128, 1792, 1792], P('sub', None, 'panel'), may hold values from -0.4 to 0.4, as said below
- neighbours: int32 [16, 131072], P(None, 'sub'), may hold values from 0 to 1792, as said below
- edge_weight: float32 [16, 131072], P(None, 'sub'), may hold values from 0.1 to 1
- node_shift: float32 [131072], P('sub'), may hold values from 3 to 12
- send_rows: int32 [128, 2, 384], P('sub'), may hold values from 0 to 1023
Outputs:
- new_solution: float32 [131072, 256], P('sub', 'panel')
- new_residual: float32 [131072, 256], P('sub', 'panel')
- step_alpha: float32 [256], P('panel')
- step_omega: float32 [256], P('panel')
- next_rho: float32 [256], P('panel')
Inputs may be any that keep to these rules, and one draw needn't show every extreme that they name: lower_inverse[s] is zero above its diagonal. upper_inverse[s] is zero below its diagonal. `neighbours`: an entry below 1024 is an owned node, from 1024 a ghost node from the lower neighbour's list, from 1408 one from the upper neighbour's list; 1792 marks an empty slot. send_rows[s, 0] lists the rows of subdomain s that subdomain s - 1 holds as ghosts, send_rows[s, 1] those that subdomain s + 1 holds, modulo 128.
All inputs are finite; a program needn't handle non-finite values.
Results may differ from a plain program's by a relative error of at most 0.0097.
Values may be sent and summed in bfloat16 or wider, within the bound.
A program may use at most 64 MiB of HBM per device.

v0:
```python
import functools

import jax
import jax.numpy as jnp
from jax import lax
from jax.sharding import Mesh
from jax.sharding import PartitionSpec as P

SUB = ("sub_0", "sub_1", "sub_2", "sub_3")


FLOOR_SHARE = 0.3
EPSILON = 1e-06


def padded_2(cells, sides, width):
    for axis, dim in sides:
        count = lax.axis_size(axis)
        head = lax.slice_in_dim(cells, 0, width, axis=dim)
        tail = lax.slice_in_dim(cells, cells.shape[dim] - width, cells.shape[dim], axis=dim)
        cells = jnp.concatenate(
            [
                lax.ppermute(tail, axis, [(i, (i + 1) % count) for i in range(count)]),
                cells,
                lax.ppermute(head, axis, [((i + 1) % count, i) for i in range(count)]),
            ],
            axis=dim,
        )
    return cells


def in_blocks(array, dim, devices):
    lengths = array.shape
    blocks = array.reshape(*lengths[:dim], devices, lengths[dim] // devices, *lengths[dim + 1 :])
    return jnp.moveaxis(blocks, dim, 0)


def sent_and_summed(array, axis, dim):
    devices = lax.axis_size(axis)
    blocks = lax.all_to_all(in_blocks(array, dim, devices), axis, 0, 0, tiled=True)
    return jnp.sum(blocks, axis=0)


def one_axis_at_a_time(array, axes):
    return functools.reduce(lax.psum, axes, array)


def extend(vector, send_rows):
    outgoing = jnp.concatenate([vector[send_rows[0, 0]], vector[send_rows[0, 1]]], axis=0)
    border = send_rows.shape[2]
    padded = padded_2(outgoing, ((SUB, 0),), border)
    return jnp.concatenate([vector, padded[:border], padded[3 * border :]], axis=0)


def operate(vector, send_rows, neighbours, edge_weight, node_shift):
    extended = extend(vector, send_rows)
    ext_rows = extended.shape[0]
    padded = jnp.concatenate([extended, jnp.zeros((1, vector.shape[1]), jnp.float32)], axis=0)
    present = jnp.where(neighbours < ext_rows, edge_weight, 0.0)
    coupled = jnp.sum(present[:, :, None] * padded[neighbours], axis=0)
    diagonal = node_shift + jnp.sum(present, axis=0)
    return diagonal[:, None] * vector - coupled


def precondition(vector, send_rows, factors):
    lower_panel, upper_panel = factors
    own_rows, local_sources = vector.shape
    rounded = extend(vector, send_rows).astype(jnp.bfloat16)
    columns = lax.all_to_all(rounded, "panel", split_axis=0, concat_axis=1, tiled=True)
    inner_part = sent_and_summed(
        jnp.dot(lower_panel, columns, preferred_element_type=jnp.float32), "panel", 0
    ).astype(jnp.bfloat16)
    partial_sum = jnp.dot(upper_panel[:own_rows], inner_part, preferred_element_type=jnp.float32)
    return sent_and_summed(partial_sum, "panel", 1)


def per_device(
    solution,
    residual,
    shadow,
    direction,
    old_image,
    rho_prev,
    alpha_prev,
    omega_prev,
    lower_inverse,
    upper_inverse,
    neighbours,
    edge_weight,
    node_shift,
    send_rows,
):
    node_count = residual.shape[0] * lax.axis_size(SUB)
    factors = (lower_inverse[0], upper_inverse[0])
    opening = (
        one_axis_at_a_time(jnp.sum(shadow * residual, axis=0), SUB),
        one_axis_at_a_time(jnp.sum(shadow * shadow, axis=0), SUB),
    )
    rho_now = opening[0] / node_count
    shadow_square = opening[1] / node_count
    step_beta = rho_now / rho_prev * (alpha_prev / omega_prev)
    new_direction = residual + step_beta * (direction - omega_prev * old_image)
    direction_hat = precondition(new_direction, send_rows, factors)
    image_new = operate(direction_hat, send_rows, neighbours, edge_weight, node_shift)
    second = (
        one_axis_at_a_time(jnp.sum(shadow * image_new, axis=0), SUB),
        one_axis_at_a_time(jnp.sum(image_new * image_new, axis=0), SUB),
    )
    denominator = second[0] / node_count
    image_square = second[1] / node_count
    step_alpha = rho_now / jnp.maximum(
        denominator, FLOOR_SHARE * jnp.sqrt(shadow_square * image_square)
    )
    middle = residual - step_alpha * image_new
    middle_hat = precondition(middle, send_rows, factors)
    tested = operate(middle_hat, send_rows, neighbours, edge_weight, node_shift)
    closing = (
        one_axis_at_a_time(jnp.sum(tested * middle, axis=0), SUB),
        one_axis_at_a_time(jnp.sum(tested * tested, axis=0), SUB),
        one_axis_at_a_time(jnp.sum(shadow * middle, axis=0), SUB),
        one_axis_at_a_time(jnp.sum(shadow * tested, axis=0), SUB),
    )
    step_omega = closing[0] / node_count / (closing[1] / node_count + EPSILON)
    new_residual = middle - step_omega * tested
    next_rho = closing[2] / node_count - step_omega * (closing[3] / node_count)
    new_solution = solution + step_alpha * direction_hat + step_omega * middle_hat
    return (new_solution, new_residual, step_alpha, step_omega, next_rho)


def solution(mesh):
    torus = Mesh(
        mesh.devices.reshape(4, 4, 4, 2, mesh.shape["panel"]),
        ("sub_0", "sub_1", "sub_2", "sub_3", "panel"),
    )
    in_specs = (
        P(SUB, "panel"),
        P(SUB, "panel"),
        P(SUB, "panel"),
        P(SUB, "panel"),
        P(SUB, "panel"),
        P("panel"),
        P("panel"),
        P("panel"),
        P(SUB, None, "panel"),
        P(SUB, None, "panel"),
        P(None, SUB),
        P(None, SUB),
        P(SUB),
        P(SUB, None, None),
    )
    out_specs = (P(SUB, "panel"), P(SUB, "panel"), P("panel"), P("panel"), P("panel"))
    return jax.shard_map(
        per_device, mesh=torus, in_specs=in_specs, out_specs=out_specs, check_vma=False
    )
```

profile of v0, /device:TPU:1, one launch (start us, length us, event | category | flops | bytes accessed | tf_op | source)
XLA Modules:
  0.0 427.7 jit_solution(668824493730074484)
XLA Ops:
  2.1 9.3 %psum.224 = f32[128]{0:T(128)S(1)} all-reduce(f32[128]{0:T(128)S(1)} %multiply_reduce_fusion.9), channel_id=1, replica_groups=mesh['sub_0'=4,'sub_1'=4,'sub_2'=4,'sub_3'=2,'panel'=2] {'sub_0'}, use_global_device_ids=true, to_apply=%region_1.0 | all-reduce | flops 128 | bytes 1024 | tf_op jit(solution)/shard_map/psum | solution.py:45
  11.4 9.0 %psum.225 = f32[128]{0:T(128)S(1)} all-reduce(f32[128]{0:T(128)S(1)} %psum.224), channel_id=1, replica_groups=mesh['sub_0'=4,'sub_1'=4,'sub_2'=4,'sub_3'=2,'panel'=2] {'sub_1'}, use_global_device_ids=true, to_apply=%region_2.0 | all-reduce | flops 128 | bytes 1024 | tf_op jit(solution)/shard_map/psum | solution.py:45
  20.4 12.9 %psum.226 = f32[128]{0:T(128)S(1)} all-reduce(f32[128]{0:T(128)S(1)} %psum.225), channel_id=1, replica_groups=mesh['sub_0'=4,'sub_1'=4,'sub_2'=4,'sub_3'=2,'panel'=2] {'sub_2'}, use_global_device_ids=true, to_apply=%region_3.0 | all-reduce | flops 128 | bytes 1024 | tf_op jit(solution)/shard_map/psum | solution.py:45
  33.3 8.6 %psum.227 = f32[128]{0:T(128)S(1)} all-reduce(f32[128]{0:T(128)S(1)} %psum.226), channel_id=1, replica_groups=mesh['sub_0'=4,'sub_1'=4,'sub_2'=4,'sub_3'=2,'panel'=2] {'sub_3'}, use_global_device_ids=true, to_apply=%region_4.0 | all-reduce | flops 128 | bytes 1024 | tf_op jit(solution)/shard_map/psum | solution.py:45
  49.2 6.3 %collective-permute-done.1 = bf16[384,128]{1,0:T(8,128)(2,1)S(1)} collective-permute-done((bf16[384,128]{1,0:T(8,128)(2,1)}, bf16[384,128]{1,0:T(8,128)(2,1)S(1)}, u32[]{:S(2)}, u32[]{:S(2)}) %collective-permute-start.1) | collective-permute-done | bytes 98336 | tf_op jit(solution)/shard_map/ppermute | solution.py:25
  59.1 8.5 %all_to_all.52 = bf16[2,896,128]{1,2,0:T(8,128)(2,1)S(1)} all-to-all(bf16[2,896,128]{1,2,0:T(8,128)(2,1)} %copy.21), channel_id=1, replica_groups=mesh['sub_0'=4,'sub_1'=4,'sub_2'=4,'sub_3'=2,'panel'=2] {'panel'}, dimensions={0} | all-to-all | bytes 917504 | tf_op jit(solution)/shard_map/all_to_all | solution.py:69
  69.0 19.2 %all_to_all.53 = f32[2,896,256]{1,2,0:T(8,128)} all-to-all(f32[2,896,256]{1,2,0:T(8,128)S(1)} %bitcast.54), channel_id=1, replica_groups=mesh['sub_0'=4,'sub_1'=4,'sub_2'=4,'sub_3'=2,'panel'=2] {'panel'}, dimensions={0} | all-to-all | bytes 3670016 | tf_op jit(solution)/shard_map/all_to_all | solution.py:40
  98.6 8.2 %all-to-all-done.2 = f32[2,1024,128]{1,2,0:T(8,128)} async-done(((f32[2,1024,128]{1,2,0:T(8,128)}), f32[2,1024,128]{1,2,0:T(8,128)}, u32[]{:S(2)}, u32[]{:S(2)}) %all-to-all-start.2) | async-done | bytes 1048608 | tf_op jit(solution)/shard_map/all_to_all | solution.py:40
  116.3 12.4 %collective-permute-start.2 = (f32[384,128]{1,0:T(8,128)}, f32[384,128]{1,0:T(8,128)S(1)}, u32[]{:S(2)}, u32[]{:S(2)}) collective-permute-start(f32[384,128]{1,0:T(8,128)} %gather_fusion.2), channel_id=1, source_target_pairs={{0,2},{2,4},{4,6},{6,8},{8,10},{10,12},{12,14},{14,16},{16,18},{18... | collective-permute-start | bytes 589832 | tf_op jit(solution)/shard_map/ppermute | solution.py:23
  138.7 55.6 %gather_fusion.4 = f32[16384,128]{1,0:T(8,128)} fusion(f32[1793,128]{1,0:T(8,128)} %maximum_maximum_fusion, s32[16384]{0:T(1024)S(1)} %broadcast_clamp_fusion), kind=kCustom, calls=%fused_computation.4 | custom fusion | bytes 16842752 | tf_op jit(solution)/shard_map/gather | solution.py:60
  194.3 5.3 %multiply_reduce_fusion.1 = f32[1024,128]{1,0:T(8,128)S(1)} fusion(f32[16,1024,128]{2,1,0:T(8,128)} %bitcast.53, f32[16,1024]{1,0:T(8,128)S(1)} %get-tuple-element.49), kind=kLoop, calls=%fused_computation.11 | loop fusion | flops 4063232 | bytes 8978432 | tf_op jit(solution)/shard_map/reduce_sum | solution.py:60
  200.7 6.2 %all-reduce.5 = (f32[128]{0:T(128)S(1)}, f32[128]{0:T(128)S(1)}, f32[128]{0:T(128)S(1)}) all-reduce(f32[128]{0:T(128)S(1)} %get-tuple-element.10, f32[128]{0:T(128)S(1)} %get-tuple-element.11, f32[128]{0:T(128)S(1)} %get-tuple-element.9), channel_id=1, replica_groups=mesh['sub_0'=4,'sub_1'=4,'sub_2'=4,'sub_3'=2,'panel'=2] {'sub_0'}, use_global_device_ids=true, to_apply=%region_20.21 | all-reduce | flops 384 | bytes 3072 | tf_op jit(solution)/shard_map/psum | solution.py:45
  206.8 6.0 %all-reduce.3 = (f32[128]{0:T(128)S(1)}, f32[128]{0:T(128)S(1)}, f32[128]{0:T(128)S(1)}) all-reduce(f32[128]{0:T(128)S(1)} %get-tuple-element.32, f32[128]{0:T(128)S(1)} %get-tuple-element.33, f32[128]{0:T(128)S(1)} %get-tuple-element.34), channel_id=1, replica_groups=mesh['sub_0'=4,'sub_1'=4,'sub_2'=4,'sub_3'=2,'panel'=2] {'sub_1'}, use_global_device_ids=true, to_apply=%region_21.22 | all-reduce | flops 384 | bytes 3072 | tf_op jit(solution)/shard_map/psum | solution.py:45
  212.8 16.4 %all-reduce.1 = (f32[128]{0:T(128)S(1)}, f32[128]{0:T(128)S(1)}, f32[128]{0:T(128)S(1)}) all-reduce(f32[128]{0:T(128)S(1)} %get-tuple-element.25, f32[128]{0:T(128)S(1)} %get-tuple-element.26, f32[128]{0:T(128)S(1)} %get-tuple-element.27), channel_id=1, replica_groups=mesh['sub_0'=4,'sub_1'=4,'sub_2'=4,'sub_3'=2,'panel'=2] {'sub_2'}, use_global_device_ids=true, to_apply=%region_22.23 | all-reduce | flops 384 | bytes 3072 | tf_op jit(solution)/shard_map/psum | solution.py:45
  250.0 8.5 %all_to_all.54 = bf16[2,896,128]{1,2,0:T(8,128)(2,1)S(1)} all-to-all(bf16[2,896,128]{1,2,0:T(8,128)(2,1)} %copy.29), channel_id=1, replica_groups=mesh['sub_0'=4,'sub_1'=4,'sub_2'=4,'sub_3'=2,'panel'=2] {'panel'}, dimensions={0} | all-to-all | bytes 917504 | tf_op jit(solution)/shard_map/all_to_all | solution.py:69
  259.8 19.9 %all_to_all.55 = f32[2,896,256]{1,2,0:T(8,128)} all-to-all(f32[2,896,256]{1,2,0:T(8,128)S(1)} %bitcast.55), channel_id=1, replica_groups=mesh['sub_0'=4,'sub_1'=4,'sub_2'=4,'sub_3'=2,'panel'=2] {'panel'}, dimensions={0} | all-to-all | bytes 3670016 | tf_op jit(solution)/shard_map/all_to_all | solution.py:40
  284.7 11.5 %all_to_all.56 = f32[2,1024,128]{1,2,0:T(8,128)} all-to-all(f32[2,1024,128]{1,2,0:T(8,128)S(1)} %bitcast.63), channel_id=1, replica_groups=mesh['sub_0'=4,'sub_1'=4,'sub_2'=4,'sub_3'=2,'panel'=2] {'panel'}, dimensions={0} | all-to-all | bytes 2097152 | tf_op jit(solution)/shard_map/all_to_all | solution.py:40
  305.7 14.1 %collective-permute-start.6 = (f32[384,128]{1,0:T(8,128)}, f32[384,128]{1,0:T(8,128)S(1)}, u32[]{:S(2)}, u32[]{:S(2)}) collective-permute-start(f32[384,128]{1,0:T(8,128)} %gather_fusion.7), channel_id=1, source_target_pairs={{0,2},{2,4},{4,6},{6,8},{8,10},{10,12},{12,14},{14,16},{16,18},{18... | collective-permute-start | bytes 589832 | tf_op jit(solution)/shard_map/ppermute | solution.py:23
  322.7 5.1 %collective-permute-done.7 = f32[384,128]{1,0:T(8,128)S(1)} collective-permute-done((f32[384,128]{1,0:T(8,128)}, f32[384,128]{1,0:T(8,128)S(1)}, u32[]{:S(2)}, u32[]{:S(2)}) %collective-permute-start.7) | collective-permute-done | bytes 196640 | tf_op jit(solution)/shard_map/ppermute | solution.py:25
  330.2 55.6 %gather_fusion.9 = f32[16384,128]{1,0:T(8,128)} fusion(f32[1793,128]{1,0:T(8,128)} %maximum_maximum_fusion.1, s32[16384]{0:T(1024)S(1)} %copy-done.7), kind=kCustom, calls=%fused_computation.9 | custom fusion | bytes 16842752 | tf_op jit(solution)/shard_map/gather | solution.py:60
  385.8 5.4 %multiply_reduce_fusion = f32[1024,128]{1,0:T(8,128)S(1)} fusion(f32[16,1024,128]{2,1,0:T(8,128)} %bitcast.52, f32[16,1024]{1,0:T(8,128)S(1)} %get-tuple-element.49), kind=kLoop, calls=%fused_computation.10 | loop fusion | flops 4063232 | bytes 8978432 | tf_op jit(solution)/shard_map/reduce_sum | solution.py:60
  392.2 8.1 %all-reduce.4 = (f32[128]{0:T(128)S(1)}, f32[128]{0:T(128)S(1)}, f32[128]{0:T(128)S(1)}, f32[128]{0:T(128)S(1)}) all-reduce(f32[128]{0:T(128)S(1)} %get-tuple-element.8, f32[128]{0:T(128)S(1)} %get-tuple-element.6, f32[128]{0:T(128)S(1)} %get-tuple-element.7, ...), channel_id=1, replica_groups=mesh['sub_0'=4,'sub_1'=4,'sub_2'=4,'sub_3'=2,'panel'=2] {'sub_0'}, use_global_device_ids=true, to_apply=%region_33.34 | all-reduce | flops 512 | bytes 4096 | tf_op jit(solution)/shard_map/psum | solution.py:45
  400.3 8.2 %all-reduce.2 = (f32[128]{0:T(128)S(1)}, f32[128]{0:T(128)S(1)}, f32[128]{0:T(128)S(1)}, f32[128]{0:T(128)S(1)}) all-reduce(f32[128]{0:T(128)S(1)} %get-tuple-element.28, f32[128]{0:T(128)S(1)} %get-tuple-element.29, f32[128]{0:T(128)S(1)} %get-tuple-element.30, ...), channel_id=1, replica_groups=mesh['sub_0'=4,'sub_1'=4,'sub_2'=4,'sub_3'=2,'panel'=2] {'sub_1'}, use_global_device_ids=true, to_apply=%region_34.35 | all-reduce | flops 512 | bytes 4096 | tf_op jit(solution)/shard_map/psum | solution.py:45
  408.5 11.4 %all-reduce = (f32[128]{0:T(128)S(1)}, f32[128]{0:T(128)S(1)}, f32[128]{0:T(128)S(1)}, f32[128]{0:T(128)S(1)}) all-reduce(f32[128]{0:T(128)S(1)} %get-tuple-element.21, f32[128]{0:T(128)S(1)} %get-tuple-element.22, f32[128]{0:T(128)S(1)} %get-tuple-element.23, ...), channel_id=1, replica_groups=mesh['sub_0'=4,'sub_1'=4,'sub_2'=4,'sub_3'=2,'panel'=2] {'sub_2'}, use_global_device_ids=true, to_apply=%region_35.36 | all-reduce | flops 512 | bytes 4096 | tf_op jit(solution)/shard_map/psum | solution.py:45
  (95 shorter events, 95.2 us)
Async XLA Ops:
  0.6 67.0 %copy-start = (bf16[1,1792,896]{2,1,0:T(8,128)(2,1)S(1)}, bf16[1,1792,896]{2,1,0:T(8,128)(2,1)}, u32[]{:S(2)}) copy-start(bf16[1,1792,896]{2,1,0:T(8,128)(2,1)} %param.22) | copy-start | bytes 9633796
  41.9 27.0 %copy-start.16 = (f32[128]{0:T(128)}, f32[128]{0:T(128)S(1)}, u32[]{:S(2)}) copy-start(f32[128]{0:T(128)S(1)} %psum.227) | copy-start | bytes 1540
  46.7 2.4 collective-permute-start
  46.9 64.1 %copy-start.10 = (s32[1024]{0:T(1024)}, s32[1024]{0:T(1024)S(1)}, u32[]{:S(2)}) copy-start(s32[1024]{0:T(1024)S(1)} %pad_clamp_fusion) | copy-start | bytes 12292
  48.8 6.6 %collective-permute-start.1 = (bf16[384,128]{1,0:T(8,128)(2,1)}, bf16[384,128]{1,0:T(8,128)(2,1)S(1)}, u32[]{:S(2)}, u32[]{:S(2)}) collective-permute-start(bf16[384,128]{1,0:T(8,128)(2,1)} %gather_fusion.1), channel_id=1, source_target_pairs={{2,0},{4,2},{6,4},{8,6},{10,8},{12,10},{14,12},{16,14},{18,16},{20... | collective-permute-start | bytes 294920 | tf_op jit(solution)/shard_map/ppermute | solution.py:25
  90.7 7.9 %copy-start.8 = (s32[16,1024]{1,0:T(8,128)S(1)}, s32[16,1024]{1,0:T(8,128)}, u32[]{:S(2)}) copy-start(s32[16,1024]{1,0:T(8,128)} %param.24) | copy-start | bytes 196612
  94.1 12.7 %all-to-all-start.2 = ((f32[2,1024,128]{1,2,0:T(8,128)}), f32[2,1024,128]{1,2,0:T(8,128)}, u32[]{:S(2)}, u32[]{:S(2)}) async-start(f32[2,1024,128]{1,2,0:T(8,128)} %bitcast.62), calls=%async_computation.2 | async-start | bytes 2097152 | tf_op jit(solution)/shard_map/all_to_all | solution.py:40
  98.5 30.2 %copy-start.9 = (f32[16,1024]{1,0:T(8,128)S(1)}, f32[16,1024]{1,0:T(8,128)}, u32[]{:S(2)}) copy-start(f32[16,1024]{1,0:T(8,128)} %param.25) | copy-start | bytes 196612
  98.6 40.1 %copy-start.6 = (s32[16384]{0:T(1024)}, s32[16384]{0:T(1024)S(1)}, u32[]{:S(2)}) copy-start(s32[16384]{0:T(1024)S(1)} %broadcast_clamp_fusion) | copy-start | bytes 196612
  98.6 30.2 %copy-start.14 = (f32[1024]{0:T(1024)S(1)}, f32[1024]{0:T(1024)}, u32[]{:S(2)}) copy-start(f32[1024]{0:T(1024)} %param.26) | copy-start | bytes 12292
  116.3 17.3 %collective-permute-start.2 = (f32[384,128]{1,0:T(8,128)}, f32[384,128]{1,0:T(8,128)S(1)}, u32[]{:S(2)}, u32[]{:S(2)}) collective-permute-start(f32[384,128]{1,0:T(8,128)} %gather_fusion.2), channel_id=1, source_target_pairs={{0,2},{2,4},{4,6},{6,8},{8,10},{10,12},{12,14},{14,16},{16,18},{18... | collective-permute-start | bytes 589832 | tf_op jit(solution)/shard_map/ppermute | solution.py:23
  128.7 7.6 %collective-permute-start.3 = (f32[384,128]{1,0:T(8,128)}, f32[384,128]{1,0:T(8,128)S(1)}, u32[]{:S(2)}, u32[]{:S(2)}) collective-permute-start(f32[384,128]{1,0:T(8,128)} %gather_fusion.3), channel_id=1, source_target_pairs={{2,0},{4,2},{6,4},{8,6},{10,8},{12,10},{14,12},{16,14},{18,16},{20... | collective-permute-start | bytes 589832 | tf_op jit(solution)/shard_map/ppermute | solution.py:25
  194.3 5.4 %copy-start.4 = (f32[1024,128]{1,0:T(8,128)S(1)}, f32[1024,128]{1,0:T(8,128)}, u32[]{:S(2)}) copy-start(f32[1024,128]{1,0:T(8,128)} %param.16) | copy-start | bytes 1572868
  194.3 37.4 %copy-start.17 = (f32[128]{0:T(128)S(1)}, f32[128]{0:T(128)}, u32[]{:S(2)}) copy-start(f32[128]{0:T(128)} %copy-done.16) | copy-start | bytes 1540
  239.8 3.3 collective-permute-start.4
  241.2 6.0 %collective-permute-start.5 = (bf16[384,128]{1,0:T(8,128)(2,1)}, bf16[384,128]{1,0:T(8,128)(2,1)S(1)}, u32[]{:S(2)}, u32[]{:S(2)}) collective-permute-start(bf16[384,128]{1,0:T(8,128)(2,1)} %gather_fusion.6), channel_id=1, source_target_pairs={{2,0},{4,2},{6,4},{8,6},{10,8},{12,10},{14,12},{16,14},{18,16},{20... | collective-permute-start | bytes 294920 | tf_op jit(solution)/shard_map/ppermute | solution.py:25
  284.7 15.7 %copy-start.11 = (s32[1024]{0:T(1024)S(1)}, s32[1024]{0:T(1024)}, u32[]{:S(2)}) copy-start(s32[1024]{0:T(1024)} %copy-done.10) | copy-start | bytes 12292
  298.3 31.8 %copy-start.7 = (s32[16384]{0:T(1024)S(1)}, s32[16384]{0:T(1024)}, u32[]{:S(2)}) copy-start(s32[16384]{0:T(1024)} %copy-done.6) | copy-start | bytes 196612
  305.7 17.0 %collective-permute-start.6 = (f32[384,128]{1,0:T(8,128)}, f32[384,128]{1,0:T(8,128)S(1)}, u32[]{:S(2)}, u32[]{:S(2)}) collective-permute-start(f32[384,128]{1,0:T(8,128)} %gather_fusion.7), channel_id=1, source_target_pairs={{0,2},{2,4},{4,6},{6,8},{8,10},{10,12},{12,14},{14,16},{16,18},{18... | collective-permute-start | bytes 589832 | tf_op jit(solution)/shard_map/ppermute | solution.py:23
  319.8 8.0 %collective-permute-start.7 = (f32[384,128]{1,0:T(8,128)}, f32[384,128]{1,0:T(8,128)S(1)}, u32[]{:S(2)}, u32[]{:S(2)}) collective-permute-start(f32[384,128]{1,0:T(8,128)} %gather_fusion.8), channel_id=1, source_target_pairs={{2,0},{4,2},{6,4},{8,6},{10,8},{12,10},{14,12},{16,14},{18,16},{20... | collective-permute-start | bytes 589832 | tf_op jit(solution)/shard_map/ppermute | solution.py:25
  385.8 5.4 %copy-start.2 = (f32[1024,128]{1,0:T(8,128)S(1)}, f32[1024,128]{1,0:T(8,128)}, u32[]{:S(2)}) copy-start(f32[1024,128]{1,0:T(8,128)} %copy.32) | copy-start | bytes 1572868
  385.8 5.4 %copy-start.3 = (f32[1024,128]{1,0:T(8,128)S(1)}, f32[1024,128]{1,0:T(8,128)}, u32[]{:S(2)}) copy-start(f32[1024,128]{1,0:T(8,128)} %get-tuple-element.46) | copy-start | bytes 1572868
  385.8 5.4 %copy-start.5 = (f32[1024,128]{1,0:T(8,128)S(1)}, f32[1024,128]{1,0:T(8,128)}, u32[]{:S(2)}) copy-start(f32[1024,128]{1,0:T(8,128)} %param.16) | copy-start | bytes 1572868
  385.8 39.1 %copy-start.13 = (f32[128]{0:T(128)S(1)}, f32[128]{0:T(128)}, u32[]{:S(2)}) copy-start(f32[128]{0:T(128)} %copy-done.12) | copy-start | bytes 1540
  (3 other events, 8.6 us)
where the time goes:
time: 429 us; the launch traced here: 428 us
  blocking collectives  171 us (40%)
  local copies, waits for them, and re-layouts  140 us (33%)
  other arithmetic  39.1 us (9%)
  waiting for transfers between devices  36.1 us (8%)
  starting transfers between devices  32.8 us (8%)
  matrix products  8.15 us (2%)
    gather x2, local copies, waits for them, and re-layouts, operate(): coupled = jnp.sum(present[:, :, None] * padded[neighbours], axis=0)  111 us
    psum x12, blocking collectives, one_axis_at_a_time(): return functools.reduce(lax.psum, axes, array)  103 us
    all_to_all x3, blocking collectives, sent_and_summed(): lax.all_to_all(in_blocks(array, dim, devices), axis, 0, 0, tiled=True)  50.6 us
    ppermute x4, starting transfers between devices, padded_2(): lax.ppermute(tail, axis, [(i, (i + 1) % count) for i in range(count)])  28 us
    ppermute x4, waiting for transfers between devices, padded_2(): lax.ppermute(head, axis, [((i + 1) % count, i) for i in range(count)])  18.1 us
    all_to_all x2, blocking collectives, precondition(): lax.all_to_all(rounded, 'panel', split_axis=0, concat_axis=1, tiled=True)  17.1 us
    reduce_sum x2, other arithmetic, operate(): coupled = jnp.sum(present[:, :, None] * padded[neighbours], axis=0)  10.7 us
    gather x4, local copies, waits for them, and re-layouts, extend(): vector[send_rows[0, 0]]  10 us
  transfers between devices with their start and end apart: 9, of which 8 were waited for; matrix products, arithmetic and copies ran while one was open for 0% of the time, Pallas kernels for 0%

commit v1 on v0

v1 whole, which is shorter than its diff:
```python
import functools

import jax
import jax.numpy as jnp
from jax import lax
from jax.experimental import pallas as pl
from jax.experimental.pallas import tpu as pltpu
from jax.sharding import Mesh
from jax.sharding import PartitionSpec as P

SUB = ("sub_0", "sub_1", "sub_2", "sub_3")
FLOOR_SHARE = 0.3
EPSILON = 1e-06

OWN = 1024
EXT = 1792
HALF = 896
BORDER = 384
NB = 16
COLS = 128
CHUNK = 128
NX, NY, NZ, NC = 4, 4, 4, 2
F32 = jnp.float32
BF16 = jnp.bfloat16
MESH = pl.DeviceIdType.MESH


def dot(a, b):
    return lax.dot_general(a, b, (((1,), (0,)), ((), ())), preferred_element_type=F32)


def dot_nt(a, b):
    return lax.dot_general(a, b, (((1,), (1,)), ((), ())), preferred_element_type=F32)


def chunks(body, init=0):
    def step(i, carry):
        return body(pl.ds(pl.multiple_of(i * CHUNK, CHUNK), CHUNK), carry)

    return lax.fori_loop(0, OWN // CHUNK, step, init)


def fold(x):
    return jnp.sum(x.reshape(CHUNK // 8, 8, COLS), axis=0)


def butterfly(x):
    sub = lax.broadcasted_iota(jnp.int32, x.shape, 0)
    lane = lax.broadcasted_iota(jnp.int32, x.shape, 1) // 16
    for s in (1, 2, 4):
        down = pltpu.roll(pltpu.roll(x, s, 0), 128 - 16 * s, 1)
        up = pltpu.roll(pltpu.roll(x, 8 - s, 0), 16 * s, 1)
        sub_bit = (sub // s) % 2
        lane_bit = (lane // s) % 2
        x = jnp.where(sub_bit == lane_bit, x, jnp.where(sub_bit == 1, down, up))
    return x


def kernel(
    r_hbm, s_hbm, d_hbm, oi_hbm, sol_hbm, low_hbm, up_hbm,
    scal, nbr, ew, shift, rows_ref,
    new_sol, new_res, alpha_out, omega_out, rho_out,
    r, s, d, oi, sol, low, up,
    w_mat, sel, diag, code_t, base_t, wgt_t,
    xe, rq, sel_rq, g_rq, sel_u, g_u, ub, y, v, m, mh,
    x1_in, x2_in, p_in, u_in, y_in, p_out, u_out, y_out, inner, part,
    ar_a, ar_b,
    load_sem, g_send, g_recv, p_send, p_recv, a_send, a_recv,
):
    panel = lax.axis_index("panel")
    ix, iy, iz, ic = (lax.axis_index(name) for name in SUB)
    flat = ((ix * NY + iy) * NZ + iz) * NC + ic

    def coords(index):
        return {
            "sub_0": index // (NY * NZ * NC),
            "sub_1": (index // (NZ * NC)) % NY,
            "sub_2": (index // NC) % NZ,
            "sub_3": index % NC,
        }

    total = NX * NY * NZ * NC
    above = coords((flat + 1) % total)
    below = coords((flat + total - 1) % total)
    partner = {"panel": 1 - panel}
    plane = [
        {"sub_0": (ix + o // NY) % NX, "sub_1": (iy + o % NY) % NY} for o in range(1, NX * NY)
    ]
    column = [
        {"sub_2": (iz + o // NC) % NZ, "sub_3": (ic + o % NC) % NC} for o in range(1, NZ * NC)
    ]

    def load(src, dst, i):
        copy = pltpu.make_async_copy(src, dst, load_sem.at[i])
        copy.start()
        return copy

    loads = [
        load(s_hbm, s, 0), load(r_hbm, r, 1), load(d_hbm, d, 2), load(oi_hbm, oi, 3),
        load(low_hbm.at[0], low, 4), load(up_hbm.at[0, pl.ds(0, OWN)], up, 5), load(sol_hbm, sol, 6),
    ]

    barrier = pltpu.get_barrier_semaphore()
    peers = plane + column + [above, below, partner]
    for peer in peers:
        pl.semaphore_signal(barrier, inc=1, device_id=peer, device_id_type=MESH)

    sends = []

    def send(src, dst, ssem, rsem, peer):
        copy = pltpu.make_async_remote_copy(
            src_ref=src, dst_ref=dst, send_sem=ssem, recv_sem=rsem,
            device_id=peer, device_id_type=MESH,
        )
        copy.start()
        return copy

    def reduce_start(n, rows):
        mine = ar_a.at[n, ix * NY + iy]
        mine[...] = jnp.concatenate(rows + [jnp.zeros((8 - len(rows), COLS), F32)], axis=0)
        for o, peer in enumerate(plane):
            sends.append(send(mine, mine, a_send.at[n, o], a_recv.at[n, o], peer))
        return sends[-len(plane):]

    def reduce_middle(n, copies):
        for copy in copies:
            copy.wait_recv()
        mine = ar_b.at[n, iz * NC + ic]
        mine[...] = jnp.sum(ar_a[n], axis=0)
        for o, peer in enumerate(column):
            k = NX * NY - 1 + o
            sends.append(send(mine, mine, a_send.at[n, k], a_recv.at[n, k], peer))
        return sends[-len(column):]

    def reduce_end(n, copies):
        for copy in copies:
            copy.wait_recv()
        return jnp.sum(ar_b[n], axis=0) * (1.0 / (OWN * total))

    def ghosts_start(src, dst, k):
        a = send(src.at[pl.ds(0, BORDER)], dst.at[pl.ds(BORDER, BORDER)], g_send.at[k, 0], g_recv.at[k, 0], below)
        b = send(src.at[pl.ds(BORDER, BORDER)], dst.at[pl.ds(0, BORDER)], g_send.at[k, 1], g_recv.at[k, 1], above)
        sends.extend([a, b])
        return [a, b]

    zero = jnp.zeros((8, COLS), F32)
    loads[0].wait()
    loads[1].wait()

    def opening(at, carry):
        sr, ss = carry
        a, b = s[at, :], r[at, :]
        return sr + fold(a * b), ss + fold(a * a)

    sr, ss = chunks(opening, (zero, zero))
    pl.semaphore_wait(barrier, len(peers))
    first = reduce_start(0, [jnp.sum(sr, axis=0, keepdims=True), jnp.sum(ss, axis=0, keepdims=True)])

    lane = lax.broadcasted_iota(jnp.int32, (CHUNK, CHUNK), 1).astype(F32)
    for n in range(2 * BORDER // CHUNK):
        side, at = n // (BORDER // CHUNK), (n % (BORDER // CHUNK)) * CHUNK
        chosen = rows_ref[0, side : side + 1, at : at + CHUNK].astype(F32)
        across = jnp.transpose(jnp.broadcast_to(chosen, (CHUNK, CHUNK)))
        for t in range(OWN // CHUNK):
            sel[n * CHUNK : (n + 1) * CHUNK, t * CHUNK : (t + 1) * CHUNK] = jnp.where(
                across == lane + float(t * CHUNK), 1.0, 0.0
            ).astype(BF16)

    loads[2].wait()
    loads[3].wait()
    omega_prev = scal[2:3, :]

    def combine(at, _):
        q = d[at, :] - omega_prev * oi[at, :]
        d[at, :] = q
        rq[at, 0:COLS] = r[at, :].astype(BF16)
        rq[at, COLS : 2 * COLS] = q.astype(BF16)
        return 0

    chunks(combine)
    sel_rq[...] = dot(sel[...], rq[...]).astype(BF16)
    rq_copies = ghosts_start(sel_rq, g_rq, 0)
    second = reduce_middle(0, first)

    valid = nbr[...] < EXT
    present = jnp.sum(jnp.where(valid, ew[...], 0.0), axis=0, keepdims=True)
    for t in range(OWN // CHUNK):
        at = slice(t * CHUNK, (t + 1) * CHUNK)
        line = present[:, at] + shift[t : t + 1, :]
        diag[at, :] = jnp.transpose(jnp.broadcast_to(line, (CHUNK, CHUNK)))
        for h in range(NB // 8):
            turned = butterfly(nbr[h * 8 : h * 8 + 8, at].astype(F32))
            turned = turned.astype(jnp.int32)
            inside = lax.broadcasted_iota(jnp.int32, (8, CHUNK), 1) % 16
            here = slice(h * CHUNK, (h + 1) * CHUNK)
            code_t[t * 8 : t * 8 + 8, here] = (turned // COLS) * 16 + inside
            base_t[t * 8 : t * 8 + 8, here] = turned % COLS
            wgt_t[t * 8 : t * 8 + 8, here] = butterfly(ew[h * 8 : h * 8 + 8, at])

    blocks = EXT // COLS
    code_row = lax.broadcasted_iota(jnp.int32, (blocks * 16, 2 * CHUNK), 0)
    base_row = lax.broadcasted_iota(jnp.int32, (COLS, 2 * CHUNK), 0)

    def build(g, _):
        one = pl.ds(g, 1)
        left = jnp.where(code_row == code_t[one, :], wgt_t[one, :], 0.0).astype(BF16)
        right = jnp.where(base_row == base_t[one, :], 1.0, 0.0).astype(BF16)
        found = dot_nt(left, right).astype(BF16)
        at = pl.ds(pl.multiple_of(g * 16, 16), 16)
        for a in range(blocks):
            w_mat[at, a * COLS : (a + 1) * COLS] = found[a * 16 : (a + 1) * 16, :]
        return 0

    lax.fori_loop(0, OWN // 16, build, 0)

    def apply(n):
        x1 = xe.at[n, pl.ds(0, HALF)]
        x2 = xe.at[n, pl.ds(HALF, HALF)]
        q4 = HALF // 2

        def link(src, dst, k):
            return pltpu.make_async_remote_copy(
                src_ref=src, dst_ref=dst, send_sem=p_send.at[n, k], recv_sem=p_recv.at[n, k],
                device_id=partner, device_id_type=MESH,
            )

        give_x1 = link(x1, x1_in.at[n], 0)
        give_x2 = link(x2, x2_in.at[n], 1)
        give_p0 = link(p_out.at[n, 0], p_in.at[n, 0], 2)
        give_p1 = link(p_out.at[n, 1], p_in.at[n, 1], 3)
        give_u = link(u_out.at[n], u_in.at[n], 4)
        give_y = link(y_out.at[n], y_in.at[n], 5)

        @pl.when(panel == 0)
        def _():
            give_x2.start()

            def lower(src, dst):
                for h in range(2):
                    at = slice(h * q4, (h + 1) * q4)
                    dst[at, :] = dot(low[HALF + h * q4 : HALF + (h + 1) * q4, :], src[...]).astype(BF16)

            def upper(src, put):
                inner[0:q4, :] = dot(low[0:q4, 0:q4], src[0:q4, :]).astype(BF16)
                inner[q4:HALF, :] = dot(low[q4:HALF, :], src[...]).astype(BF16)
                put(slice(0, q4), dot(up[0:q4, :], inner[...]))
                put(slice(q4, HALF), dot(up[q4:HALF, q4:HALF], inner[q4:HALF, :]))

            lower(x1, p_out.at[n, 0])
            give_p0.start()

            def keep(at, value):
                y[at, :] = value

            upper(x1, keep)
            give_x1.wait_recv()
            lower(x1_in.at[n], p_out.at[n, 1])
            give_p1.start()

            def post(at, value):
                u_out[n, at, :] = value.astype(BF16)

            upper(x1_in.at[n], post)
            give_u.start()
            give_y.wait_recv()
            y[0:HALF, :] = y[0:HALF, :] + y_in[n, 0:HALF, :].astype(F32)
            y[HALF:OWN, :] = y_in[n, HALF:OWN, :].astype(F32)
            for copy in (give_x2, give_p0, give_p1, give_u):
                copy.wait_send()

        @pl.when(panel == 1)
        def _():
            give_x1.start()

            def lower(src, k):
                part[k, 0:q4, :] = dot(low[HALF : HALF + q4, 0:q4], src[0:q4, :])
                part[k, q4:HALF, :] = dot(low[HALF + q4 : EXT, :], src[...])

            def upper(k, put):
                inner[...] = (part[k] + p_in[n, k].astype(F32)).astype(BF16)
                for h in range(2):
                    at = slice(h * (OWN // 2), (h + 1) * (OWN // 2))
                    put(at, dot(up[at, :], inner[...]))

            lower(x2, 1)
            give_x2.wait_recv()
            lower(x2_in.at[n], 0)
            give_p0.wait_recv()

            def post(at, value):
                y_out[n, at, :] = value.astype(BF16)

            upper(0, post)
            give_y.start()
            give_p1.wait_recv()

            def keep(at, value):
                y[at, :] = value

            upper(1, keep)
            give_u.wait_recv()
            y[0:HALF, :] = y[0:HALF, :] + u_in[n].astype(F32)
            for copy in (give_x1, give_y):
                copy.wait_send()

    def operate(n, out):
        ub[...] = y[...].astype(BF16)
        sel_u[n] = dot(sel[...], ub[...]).astype(BF16)
        copies = ghosts_start(sel_u.at[n], g_u.at[n], 1 + n)
        out[...] = diag[...] * y[...] - dot(w_mat[:, 0:OWN], ub[...])
        for copy in copies:
            copy.wait_recv()
        out[...] = out[...] - dot(w_mat[:, OWN:EXT], g_u[n])

    mean = reduce_end(0, second)
    rho_now, shadow_square = mean[0:1, :], mean[1:2, :]
    step_beta = rho_now / scal[0:1, :] * (scal[1:2, :] / omega_prev)

    def direct(at, _):
        xe[0, at, :] = (r[at, :] + step_beta * d[at, :]).astype(BF16)
        return 0

    chunks(direct)
    for copy in rq_copies:
        copy.wait_recv()
    xe[0, OWN:EXT, :] = (
        g_rq[:, 0:COLS].astype(F32) + step_beta * g_rq[:, COLS : 2 * COLS].astype(F32)
    ).astype(BF16)
    loads[4].wait()
    loads[5].wait()
    apply(0)
    operate(0, v)

    def image(at, carry):
        sv, vv = carry
        a, b = s[at, :], v[at, :]
        return sv + fold(a * b), vv + fold(b * b)

    sv, vv = chunks(image, (zero, zero))
    first = reduce_start(1, [jnp.sum(sv, axis=0, keepdims=True), jnp.sum(vv, axis=0, keepdims=True)])
    ub[...] = v[...].astype(BF16)
    sel_u[2] = dot(sel[...], ub[...]).astype(BF16)
    v_copies = ghosts_start(sel_u.at[2], g_u.at[2], 3)
    loads[6].wait()
    second = reduce_middle(1, first)
    for copy in v_copies:
        copy.wait_recv()
    mean = reduce_end(1, second)
    denominator, image_square = mean[0:1, :], mean[1:2, :]
    step_alpha = rho_now / jnp.maximum(
        denominator, FLOOR_SHARE * jnp.sqrt(shadow_square * image_square)
    )
    alpha_out[...] = step_alpha

    def halfway(at, _):
        value = r[at, :] - step_alpha * v[at, :]
        m[at, :] = value
        xe[1, at, :] = value.astype(BF16)
        sol[at, :] = sol[at, :] + step_alpha * y[at, :]
        return 0

    chunks(halfway)
    xe[1, OWN:EXT, :] = (
        g_rq[:, 0:COLS].astype(F32) - step_alpha * g_u[2].astype(F32)
    ).astype(BF16)
    apply(1)
    operate(1, v)

    def closing(at, carry):
        a, b, c = s[at, :], v[at, :], m[at, :]
        tm, tt, sm, st = carry
        return tm + fold(b * c), tt + fold(b * b), sm + fold(a * c), st + fold(a * b)

    sums = chunks(closing, (zero, zero, zero, zero))
    first = reduce_start(2, [jnp.sum(x, axis=0, keepdims=True) for x in sums])
    second = reduce_middle(2, first)
    mean = reduce_end(2, second)
    step_omega = mean[0:1, :] / (mean[1:2, :] + EPSILON)
    omega_out[...] = step_omega
    rho_out[...] = mean[2:3, :] - step_omega * mean[3:4, :]

    def final(at, _):
        new_sol[at, :] = sol[at, :] + step_omega * y[at, :]
        new_res[at, :] = m[at, :] - step_omega * v[at, :]
        return 0

    chunks(final)
    for copy in sends:
        copy.wait_send()


def per_device(
    solution, residual, shadow, direction, old_image, rho_prev, alpha_prev, omega_prev,
    lower_inverse, upper_inverse, neighbours, edge_weight, node_shift, send_rows,
):
    hbm = pl.BlockSpec(memory_space=pl.ANY)
    vmem = pl.BlockSpec(memory_space=pltpu.VMEM)
    vec = pltpu.VMEM((OWN, COLS), F32)
    scal = jnp.stack([rho_prev, alpha_prev, omega_prev])
    dma = pltpu.SemaphoreType.DMA
    outs = pl.pallas_call(
        kernel,
        out_shape=[jax.ShapeDtypeStruct((OWN, COLS), F32)] * 2 + [jax.ShapeDtypeStruct((1, COLS), F32)] * 3,
        in_specs=[hbm] * 7 + [vmem] * 5,
        out_specs=[vmem] * 5,
        scratch_shapes=[vec] * 5
        + [pltpu.VMEM((EXT, HALF), BF16), pltpu.VMEM((OWN, HALF), BF16)]
        + [
            pltpu.VMEM((OWN, EXT), BF16),
            pltpu.VMEM((2 * BORDER, OWN), BF16),
            vec,
            pltpu.VMEM((OWN // 16, 256), jnp.int32),
            pltpu.VMEM((OWN // 16, 256), jnp.int32),
            pltpu.VMEM((OWN // 16, 256), F32),
        ]
        + [
            pltpu.VMEM((2, EXT, COLS), BF16),
            pltpu.VMEM((OWN, 2 * COLS), BF16),
            pltpu.VMEM((2 * BORDER, 2 * COLS), BF16),
            pltpu.VMEM((2 * BORDER, 2 * COLS), BF16),
            pltpu.VMEM((3, 2 * BORDER, COLS), BF16),
            pltpu.VMEM((3, 2 * BORDER, COLS), BF16),
            pltpu.VMEM((OWN, COLS), BF16),
            vec, vec, vec, vec,
        ]
        + [
            pltpu.VMEM((2, HALF, COLS), BF16),
            pltpu.VMEM((2, HALF, COLS), BF16),
            pltpu.VMEM((2, 2, HALF, COLS), BF16),
            pltpu.VMEM((2, HALF, COLS), BF16),
            pltpu.VMEM((2, OWN, COLS), BF16),
            pltpu.VMEM((2, 2, HALF, COLS), BF16),
            pltpu.VMEM((2, HALF, COLS), BF16),
            pltpu.VMEM((2, OWN, COLS), BF16),
            pltpu.VMEM((HALF, COLS), BF16),
            pltpu.VMEM((2, HALF, COLS), F32),
            pltpu.VMEM((3, NX * NY, 8, COLS), F32),
            pltpu.VMEM((3, NZ * NC, 8, COLS), F32),
        ]
        + [dma((7,)), dma((4, 2)), dma((4, 2)), dma((2, 6)), dma((2, 6)), dma((3, 22)), dma((3, 22))],
        compiler_params=pltpu.CompilerParams(
            collective_id=0, has_side_effects=True, vmem_limit_bytes=60 * 1024 * 1024
        ),
        name="iteration",
    )(
        residual, shadow, direction, old_image, solution, lower_inverse, upper_inverse,
        scal, neighbours, edge_weight, node_shift.reshape(OWN // CHUNK, CHUNK), send_rows,
    )
    new_solution, new_residual, alpha, omega, rho = outs
    return new_solution, new_residual, alpha[0], omega[0], rho[0]


def solution(mesh):
    torus = Mesh(
        mesh.devices.reshape(4, 4, 4, 2, mesh.shape["panel"]),
        ("sub_0", "sub_1", "sub_2", "sub_3", "panel"),
    )
    vec = P(SUB, "panel")
    one = P("panel")
    factor = P(SUB, None, "panel")
    in_specs = (
        vec, vec, vec, vec, vec, one, one, one, factor, factor,
        P(None, SUB), P(None, SUB), P(SUB), P(SUB, None, None),
    )
    return jax.shard_map(
        per_device, mesh=torus, in_specs=in_specs, out_specs=(vec, vec, one, one, one), check_vma=False
    )
```

time: 429 us -> 114 us (0.27)
  blocking collectives: 171 us -> 0 us
  local copies, waits for them, and re-layouts: 140 us -> 7.16 us
  Pallas kernels: 0 us -> 104 us
  other arithmetic: 39.1 us -> 1.27 us
  waiting for transfers between devices: 36.1 us -> 0 us
  starting transfers between devices: 32.8 us -> 0 us
  matrix products: 8.15 us -> 0 us
    gather x10 -> x0, local copies, waits for them, and re-layouts: 131 us -> none  [the longest x2 111 us: operate(): coupled = jnp.sum(present[:, :, None] * padded[neighbours], axis=0)]
    pallas_call x0 -> x1, Pallas kernels: none -> 104 us  [per_device(): pl.pallas_call(kernel, out_shape=[jax.ShapeDtypeStruct((OWN, COLS), F32)]...]
    psum x12 -> x0, blocking collectives: 103 us -> none  [one_axis_at_a_time(): return functools.reduce(lax.psum, axes, array)]
    all_to_all x5 -> x0, blocking collectives: 67.6 us -> none  [the longest x3 50.6 us: sent_and_summed(): lax.all_to_all(in_blocks(array, dim, devices), axis, 0, 0, tiled=True)]
    ppermute x8 -> x0, starting transfers between devices: 28.4 us -> none  [the longest x4 28 us: padded_2(): lax.ppermute(tail, axis, [(i, (i + 1) % count) for i in range(count)])]
    ppermute x8 -> x0, waiting for transfers between devices: 27.9 us -> none  [the longest x4 18.1 us: padded_2(): lax.ppermute(head, axis, [((i + 1) % count, i) for i in range(count)])]
    reduce_sum x10 -> x0, other arithmetic: 23.6 us -> none  [the longest x2 10.7 us: operate(): coupled = jnp.sum(present[:, :, None] * padded[neighbours], axis=0)]
    all_to_all x1 -> x0, waiting for transfers between devices: 8.21 us -> none  [sent_and_summed(): lax.all_to_all(in_blocks(array, dim, devices), axis, 0, 0, tiled=True)]
  transfers between devices with their start and end apart: 9 -> 0, of which waited for: 8 -> 0; matrix products, arithmetic and copies ran while one was open for 0% -> 0% of each run, Pallas kernels for 0% -> 0%
where the time goes in v1:
time: 114 us; the launch traced here: 113 us
  Pallas kernels  104 us (91%)
  local copies, waits for them, and re-layouts  7.16 us (6%)
  other arithmetic  1.27 us (1%)
    pallas_call x1, Pallas kernels, per_device(): pl.pallas_call(kernel, out_shape=[jax.ShapeDtypeStruct((OWN, COLS), F32)]...  104 us
    unnamed x5, local copies, waits for them, and re-layouts  7.16 us

profile of v1, /device:TPU:1, one launch (start us, length us, event | category | flops | bytes accessed | tf_op | source)
XLA Modules:
  0.0 113.4 jit_solution(13654554796127435162)
XLA Ops:
  0.6 1.3 %pad_maximum_fusion.scal = f32[3,128]{1,0:T(4,128)} fusion(f32[1,128]{1,0:T(1,128)} %bitcast.8, f32[1,128]{1,0:T(1,128)} %bitcast.9, f32[1,128]{1,0:T(1,128)} %bitcast.10), kind=kLoop, calls=%fused_computation | loop fusion | flops 768 | bytes 3072 | tf_op jit(solution)/shard_map/stack | solution.py:399
  1.9 104.3 %iteration.1 = (f32[1024,128]{1,0:T(8,128)}, f32[1024,128]{1,0:T(8,128)}, f32[1,128]{1,0:T(1,128)}, f32[1,128]{1,0:T(1,128)}, f32[1,128]{1,0:T(1,128)}) custom-call(f32[1024,128]{1,0:T(8,128)} %r_hbm.1, f32[1024,128]{1,0:T(8,128)} %s_hbm.1, f32[1024,128]{1,0:T(8,128)} %d_hbm.1, f32[1024,128]{1,0:T(8,128)} %oi_hbm.1, f32[1024,128]{1,0:T(8,128)} %sol_hbm.1, ...), custom_call_target="tpu_custom_call" | custom-call | tf_op jit(solution)/shard_map/iteration/pallas_call | solution.py:401
  106.2 1.9 %copy.24 = f32[1024,128]{1,0:T(8,128)} copy(f32[1024,128]{1,0:T(8,128)} %get-tuple-element.20) | data formatting | bytes 1048576
  108.1 1.9 %copy.25 = f32[1024,128]{1,0:T(8,128)} copy(f32[1024,128]{1,0:T(8,128)} %get-tuple-element.21) | data formatting | bytes 1048576
  110.0 1.1 copy.26
  111.1 1.1 %copy.27 = f32[128]{0:T(128)} copy(f32[128]{0:T(128)} %bitcast.12) | data formatting | bytes 1024
  112.2 1.2 %copy.28 = f32[128]{0:T(128)} copy(f32[128]{0:T(128)} %bitcast.11) | data formatting | bytes 1024

commit v2 on v1

v2 whole, which is shorter than its diff:
```python
import functools

import jax
import jax.numpy as jnp
from jax import lax
from jax.experimental import pallas as pl
from jax.experimental.pallas import tpu as pltpu
from jax.sharding import Mesh
from jax.sharding import PartitionSpec as P

SUB = ("sub_0", "sub_1", "sub_2", "sub_3")
FLOOR_SHARE = 0.3
EPSILON = 1e-06

OWN = 1024
EXT = 1792
HALF = 896
BORDER = 384
NB = 16
COLS = 128
CHUNK = 128
NX, NY, NZ, NC = 4, 4, 4, 2
F32 = jnp.float32
BF16 = jnp.bfloat16
MESH = pl.DeviceIdType.MESH


def dot(a, b):
    return lax.dot_general(a, b, (((1,), (0,)), ((), ())), preferred_element_type=F32)


def dot_nt(a, b):
    return lax.dot_general(a, b, (((1,), (1,)), ((), ())), preferred_element_type=F32)


def chunks(body, init=0):
    def step(i, carry):
        return body(pl.ds(pl.multiple_of(i * CHUNK, CHUNK), CHUNK), carry)

    return lax.fori_loop(0, OWN // CHUNK, step, init)


def fold(x):
    return jnp.sum(x.reshape(CHUNK // 8, 8, COLS), axis=0)


def butterfly(x):
    sub = lax.broadcasted_iota(jnp.int32, x.shape, 0)
    lane = lax.broadcasted_iota(jnp.int32, x.shape, 1) // 16
    for s in (1, 2, 4):
        down = pltpu.roll(pltpu.roll(x, s, 0), 128 - 16 * s, 1)
        up = pltpu.roll(pltpu.roll(x, 8 - s, 0), 16 * s, 1)
        sub_bit = (sub // s) % 2
        lane_bit = (lane // s) % 2
        x = jnp.where(sub_bit == lane_bit, x, jnp.where(sub_bit == 1, down, up))
    return x


def kernel(
    r_hbm, s_hbm, d_hbm, oi_hbm, sol_hbm, low_hbm, up_hbm,
    rho_prev, alpha_prev, omega_prev, nbr, ew, shift, rows_ref,
    sol_out, y_out_hbm, m_out, t_out, stats,
    r, s, d, oi, sol, low, up,
    w_mat, sel, diag, code_t, base_t, wgt_t,
    xe, rq, sel_rq, g_rq, sel_u, g_u, g_v, ub, vb, y, v, m,
    x1_in, r1_in, v1_in, tail_in, p_in, u_in, y_in, p_out, u_out, y_out, inner, part, x1_c, x2_c,
    step_own, step_in, ar_a, ar_b,
    load_sem, g_send, g_recv, h_send, h_recv, p_send, p_recv, a_send, a_recv,
):
    panel = lax.axis_index("panel")
    ix, iy, iz, ic = (lax.axis_index(name) for name in SUB)
    flat = ((ix * NY + iy) * NZ + iz) * NC + ic

    def coords(index):
        return {
            "sub_0": index // (NY * NZ * NC),
            "sub_1": (index // (NZ * NC)) % NY,
            "sub_2": (index // NC) % NZ,
            "sub_3": index % NC,
        }

    total = NX * NY * NZ * NC
    above = coords((flat + 1) % total)
    below = coords((flat + total - 1) % total)
    above_one = {**above, "panel": 1}
    below_one = {**below, "panel": 1}
    partner = {"panel": 1 - panel}
    plane = [
        {"sub_0": (ix + o // NY) % NX, "sub_1": (iy + o % NY) % NY} for o in range(1, NX * NY)
    ]
    column = [
        {"sub_2": (iz + o // NC) % NZ, "sub_3": (ic + o % NC) % NC} for o in range(1, NZ * NC)
    ]

    def load(src, dst, i):
        copy = pltpu.make_async_copy(src, dst, load_sem.at[i])
        copy.start()
        return copy

    loads = [
        load(s_hbm, s, 0), load(r_hbm, r, 1), load(d_hbm, d, 2), load(oi_hbm, oi, 3),
        load(low_hbm.at[0], low, 4), load(up_hbm.at[0, pl.ds(0, OWN)], up, 5), load(sol_hbm, sol, 6),
    ]

    barrier = pltpu.get_barrier_semaphore()
    peers = plane + column + [
        above, below, {**above, "panel": 1 - panel}, {**below, "panel": 1 - panel}, partner,
    ]
    for peer in peers:
        pl.semaphore_signal(barrier, inc=1, device_id=peer, device_id_type=MESH)

    sends = []

    def remote(src, dst, ssem, rsem, peer):
        return pltpu.make_async_remote_copy(
            src_ref=src, dst_ref=dst, send_sem=ssem, recv_sem=rsem,
            device_id=peer, device_id_type=MESH,
        )

    def send(src, dst, ssem, rsem, peer):
        copy = remote(src, dst, ssem, rsem, peer)
        copy.start()
        sends.append(copy)

    def all_of(buf, n, stage, count):
        every = buf.at[n, pl.ds(0, count)]
        return remote(every, every, a_send.at[n, stage], a_recv.at[n, stage], partner)

    def reduce_start(n, rows):
        mine = ar_a.at[n, ix * NY + iy]
        mine[...] = jnp.concatenate(rows + [jnp.zeros((8 - len(rows), COLS), F32)], axis=0)
        for peer in plane:
            remote(mine, mine, a_send.at[n, 0], a_recv.at[n, 0], peer).start()
        sends.append(all_of(ar_a, n, 0, NX * NY - 1))

    def reduce_middle(n):
        all_of(ar_a, n, 0, NX * NY - 1).wait_recv()
        mine = ar_b.at[n, iz * NC + ic]
        mine[...] = jnp.sum(ar_a[n], axis=0)
        for peer in column:
            remote(mine, mine, a_send.at[n, 1], a_recv.at[n, 1], peer).start()
        sends.append(all_of(ar_b, n, 1, NZ * NC - 1))

    def reduce_end(n):
        all_of(ar_b, n, 1, NZ * NC - 1).wait_recv()
        return jnp.sum(ar_b[n], axis=0) * (1.0 / (OWN * total))

    low_rows, high_rows = pl.ds(0, BORDER), pl.ds(BORDER, BORDER)

    def ghosts_to_one(src, dst, k):
        send(src.at[low_rows], dst.at[panel, high_rows], h_send.at[k, 0], h_recv.at[k, panel, 0], below_one)
        send(src.at[high_rows], dst.at[panel, low_rows], h_send.at[k, 1], h_recv.at[k, panel, 1], above_one)

    def ghosts_at_one(dst, k, c):
        remote(dst.at[c, high_rows], dst.at[c, high_rows], h_send.at[k, 0], h_recv.at[k, c, 0], partner).wait_recv()
        remote(dst.at[c, low_rows], dst.at[c, low_rows], h_send.at[k, 1], h_recv.at[k, c, 1], partner).wait_recv()

    zero = jnp.zeros((8, COLS), F32)

    lane = lax.broadcasted_iota(jnp.int32, (CHUNK, CHUNK), 1).astype(F32)
    for n in range(2 * BORDER // CHUNK):
        side, at = n // (BORDER // CHUNK), (n % (BORDER // CHUNK)) * CHUNK
        chosen = rows_ref[0, side : side + 1, at : at + CHUNK].astype(F32)
        across = jnp.transpose(jnp.broadcast_to(chosen, (CHUNK, CHUNK)))
        for t in range(OWN // CHUNK):
            sel[n * CHUNK : (n + 1) * CHUNK, t * CHUNK : (t + 1) * CHUNK] = jnp.where(
                across == lane + float(t * CHUNK), 1.0, 0.0
            ).astype(BF16)

    loads[0].wait()
    loads[1].wait()

    def opening(at, carry):
        sr, ss = carry
        a, b = s[at, :], r[at, :]
        return sr + fold(a * b), ss + fold(a * a)

    sr, ss = chunks(opening, (zero, zero))
    pl.semaphore_wait(barrier, len(peers))
    reduce_start(0, [jnp.sum(sr, axis=0, keepdims=True), jnp.sum(ss, axis=0, keepdims=True)])

    loads[2].wait()
    loads[3].wait()
    omega_before = omega_prev[...]

    def combine(at, _):
        q = d[at, :] - omega_before * oi[at, :]
        d[at, :] = q
        rq[at, 0:COLS] = r[at, :].astype(BF16)
        rq[at, COLS : 2 * COLS] = q.astype(BF16)
        return 0

    chunks(combine)
    sel_rq[...] = dot(sel[...], rq[...]).astype(BF16)
    ghosts_to_one(sel_rq, g_rq, 0)

    def link(src, dst, n, k):
        return remote(src, dst, p_send.at[n, k], p_recv.at[n, k], partner)

    give_r1 = link(rq.at[pl.ds(0, HALF), pl.ds(0, COLS)], r1_in, 0, 7)
    give_v1 = link(vb.at[pl.ds(0, HALF)], v1_in, 1, 7)

    @pl.when(panel == 1)
    def _():
        give_r1.start()

    reduce_middle(0)

    valid = nbr[...] < EXT
    present = jnp.sum(jnp.where(valid, ew[...], 0.0), axis=0, keepdims=True)
    for t in range(OWN // CHUNK):
        at = slice(t * CHUNK, (t + 1) * CHUNK)
        line = present[:, at] + shift[t : t + 1, :]
        diag[at, :] = jnp.transpose(jnp.broadcast_to(line, (CHUNK, CHUNK)))
        for h in range(NB // 8):
            turned = butterfly(nbr[h * 8 : h * 8 + 8, at].astype(F32))
            turned = turned.astype(jnp.int32)
            inside = lax.broadcasted_iota(jnp.int32, (8, CHUNK), 1) % 16
            here = slice(h * CHUNK, (h + 1) * CHUNK)
            code_t[t * 8 : t * 8 + 8, here] = (turned // COLS) * 16 + inside
            base_t[t * 8 : t * 8 + 8, here] = turned % COLS
            wgt_t[t * 8 : t * 8 + 8, here] = butterfly(ew[h * 8 : h * 8 + 8, at])

    blocks = EXT // COLS
    code_row = lax.broadcasted_iota(jnp.int32, (blocks * 16, 2 * CHUNK), 0)
    base_row = lax.broadcasted_iota(jnp.int32, (COLS, 2 * CHUNK), 0)

    def build(g, _):
        one = pl.ds(g, 1)
        left = jnp.where(code_row == code_t[one, :], wgt_t[one, :], 0.0).astype(BF16)
        right = jnp.where(base_row == base_t[one, :], 1.0, 0.0).astype(BF16)
        found = dot_nt(left, right).astype(BF16)
        at = pl.ds(pl.multiple_of(g * 16, 16), 16)
        for a in range(blocks):
            w_mat[at, a * COLS : (a + 1) * COLS] = found[a * 16 : (a + 1) * 16, :]
        return 0

    groups = OWN // 16

    def fill(n, k):
        if n == 0:
            lax.fori_loop(k * groups // 4, (k + 1) * groups // 4, build, 0)

    q4 = HALF // 2

    def apply(n):
        tail = xe.at[n, pl.ds(HALF, OWN - HALF)]
        give_x1 = link(xe.at[n, pl.ds(0, HALF)], x1_in, n, 0)
        give_tail = link(tail, tail_in.at[n], n, 1)
        give_p0 = link(p_out.at[n, 0], p_in.at[n, 0], n, 2)
        give_p1 = link(p_out.at[n, 1], p_in.at[n, 1], n, 3)
        give_u = link(u_out.at[n], u_in.at[n], n, 4)
        give_y = link(y_out.at[n], y_in.at[n], n, 5)
        give_step = link(step_own.at[n], step_in.at[n], n, 6)

        @pl.when(panel == 0)
        def _():
            give_step.start()
            give_tail.start()

            def lower(src, dst):
                for h in range(2):
                    at = slice(h * q4, (h + 1) * q4)
                    dst[at, :] = dot(low[HALF + h * q4 : HALF + (h + 1) * q4, :], src[...]).astype(BF16)

            def upper(src, put):
                inner[0:q4, :] = dot(low[0:q4, 0:q4], src[0:q4, :]).astype(BF16)
                inner[q4:HALF, :] = dot(low[q4:HALF, :], src[...]).astype(BF16)
                put(slice(0, q4), dot(up[0:q4, :], inner[...]))
                put(slice(q4, HALF), dot(up[q4:HALF, q4:HALF], inner[q4:HALF, :]))

            x1 = xe.at[n, pl.ds(0, HALF)]
            lower(x1, p_out.at[n, 0])
            give_p0.start()

            def keep(at, value):
                y[at, :] = value

            def post(at, value):
                u_out[n, at, :] = value.astype(BF16)

            if n == 0:
                upper(x1, keep)
                fill(n, 0)
                give_x1.wait_recv()
                other = x1_in
            else:
                give_r1.wait_recv()
                give_v1.wait_recv()
                give_step.wait_recv()
                x1_c[...] = (
                    r1_in[...].astype(F32) - step_in[n, 0:1, :] * v1_in[...].astype(F32)
                ).astype(BF16)
                other = x1_c
            lower(other, p_out.at[n, 1])
            give_p1.start()
            upper(other, post)
            give_u.start()
            if n == 1:
                upper(x1, keep)
            for k in (1, 2, 3):
                fill(n, k)
            give_y.wait_recv()
            for t in range(OWN // CHUNK):
                at = slice(t * CHUNK, (t + 1) * CHUNK)
                value = y_in[n, at, :].astype(F32)
                if t < HALF // CHUNK:
                    value = value + y[at, :]
                y[at, :] = value
                ub[at, :] = value.astype(BF16)
            for copy in (give_step, give_tail, give_p0, give_p1, give_u):
                copy.wait_send()

        @pl.when(panel == 1)
        def _():
            if n == 0:
                give_x1.start()
            else:
                give_step.start()

            def extended(c, own_tail, step):
                x2_c[c, 0 : OWN - HALF, :] = own_tail
                g_r = g_rq[c, :, 0:COLS].astype(F32)
                if n == 0:
                    value = g_r + step * g_rq[c, :, COLS : 2 * COLS].astype(F32)
                else:
                    value = g_r - step * g_v[c].astype(F32)
                x2_c[c, OWN - HALF : HALF, :] = value.astype(BF16)
                part[c, 0:q4, :] = dot(low[HALF : HALF + q4, 0:q4], x2_c[c, 0:q4, :])
                part[c, q4:HALF, :] = dot(low[HALF + q4 : EXT, :], x2_c[c])

            def upper(k, put):
                inner[...] = (part[k] + p_in[n, k].astype(F32)).astype(BF16)
                for h in range(2):
                    at = slice(h * (OWN // 2), (h + 1) * (OWN // 2))
                    put(at, dot(up[at, :], inner[...]))

            received = g_rq if n == 0 else g_v
            fill(n, 0)
            ghosts_at_one(received, n, 1)
            extended(1, xe[n, HALF:OWN, :], step_own[n, 0:1, :])
            ghosts_at_one(received, n, 0)
            give_step.wait_recv()
            give_tail.wait_recv()
            extended(0, tail_in[n], step_in[n, 0:1, :])
            fill(n, 1)
            give_p0.wait_recv()

            def post(at, value):
                y_out[n, at, :] = value.astype(BF16)

            upper(0, post)
            give_y.start()
            fill(n, 2)
            give_p1.wait_recv()

            def keep(at, value):
                y[at, :] = value

            upper(1, keep)
            fill(n, 3)
            give_u.wait_recv()
            for t in range(OWN // CHUNK):
                at = slice(t * CHUNK, (t + 1) * CHUNK)
                value = y[at, :]
                if t < HALF // CHUNK:
                    value = value + u_in[n, at, :].astype(F32)
                y[at, :] = value
                ub[at, :] = value.astype(BF16)
            give_y.wait_send()
            if n == 0:
                give_x1.wait_send()
                give_r1.wait_send()
            else:
                give_step.wait_send()
                give_v1.wait_send()

    def operate(n, use):
        sel_u[n, 0:BORDER, :] = dot(sel[0:BORDER, :], ub[...]).astype(BF16)
        send(sel_u.at[n, low_rows], g_u.at[n, high_rows], g_send.at[n, 0], g_recv.at[n, 0], below)
        sel_u[n, BORDER:, :] = dot(sel[BORDER:, :], ub[...]).astype(BF16)
        send(sel_u.at[n, high_rows], g_u.at[n, low_rows], g_send.at[n, 1], g_recv.at[n, 1], above)
        copies = sends[-2:]
        v[...] = diag[...] * y[...] - dot(w_mat[:, 0:OWN], ub[...])
        for copy in copies:
            copy.wait_recv()
        for h in range(2):
            at = slice(h * (OWN // 2), (h + 1) * (OWN // 2))
            use(at, v[at, :] - dot(w_mat[at, OWN:EXT], g_u[n]))

    def whole(x):
        return jnp.sum(x, axis=0, keepdims=True)

    mean = reduce_end(0)
    rho_now, shadow_square = mean[0:1, :], mean[1:2, :]
    step_beta = rho_now / rho_prev[...] * (alpha_prev[...] / omega_before)
    step_own[0] = jnp.broadcast_to(step_beta, (8, COLS))

    def direct(at, _):
        xe[0, at, :] = (r[at, :] + step_beta * d[at, :]).astype(BF16)
        return 0

    chunks(direct)
    loads[4].wait()
    loads[5].wait()
    apply(0)

    sums = []

    def image(at, value):
        v[at, :] = value
        vb[at, :] = value.astype(BF16)
        sums.append((whole(s[at, :] * value), whole(value * value)))

    operate(0, image)
    reduce_start(1, [sums[0][i] + sums[1][i] for i in range(2)])

    @pl.when(panel == 1)
    def _():
        give_v1.start()

    sel_u[2] = dot(sel[...], vb[...]).astype(BF16)
    ghosts_to_one(sel_u.at[2], g_v, 1)
    loads[6].wait()
    reduce_middle(1)
    mean = reduce_end(1)
    denominator, image_square = mean[0:1, :], mean[1:2, :]
    step_alpha = rho_now / jnp.maximum(
        denominator, FLOOR_SHARE * jnp.sqrt(shadow_square * image_square)
    )
    step_own[1] = jnp.broadcast_to(step_alpha, (8, COLS))

    def halfway(at, carry):
        value = r[at, :] - step_alpha * v[at, :]
        m[at, :] = value
        xe[1, at, :] = value.astype(BF16)
        sol[at, :] = sol[at, :] + step_alpha * y[at, :]
        return carry + fold(s[at, :] * value)

    shadow_middle = chunks(halfway, zero)
    store = [load(sol, sol_out, 7), load(m, m_out, 8)]
    apply(1)
    store.append(load(y, y_out_hbm, 9))
    sums = []

    def test(at, value):
        v[at, :] = value
        sums.append((whole(value * m[at, :]), whole(value * value), whole(s[at, :] * value)))

    operate(1, test)
    store.append(load(v, t_out, 10))
    tm, tt, st = (sums[0][i] + sums[1][i] for i in range(3))
    reduce_start(2, [tm, tt, whole(shadow_middle), st])
    reduce_middle(2)
    mean = reduce_end(2)
    stats[...] = jnp.concatenate([mean[0:4, :], step_alpha, jnp.zeros((3, COLS), F32)], axis=0)
    for copy in store:
        copy.wait()
    for copy in sends:
        copy.wait_send()


def finish(sol, y, m, t, stats, new_sol, new_res, alpha, omega, rho):
    step_omega = stats[0:1, :] / (stats[1:2, :] + EPSILON)
    new_sol[...] = sol[...] + step_omega * y[...]
    new_res[...] = m[...] - step_omega * t[...]
    alpha[...] = stats[4:5, :]
    omega[...] = step_omega
    rho[...] = stats[2:3, :] - step_omega * stats[3:4, :]


def per_device(
    solution, residual, shadow, direction, old_image, rho_prev, alpha_prev, omega_prev,
    lower_inverse, upper_inverse, neighbours, edge_weight, node_shift, send_rows,
):
    hbm = pl.BlockSpec(memory_space=pl.ANY)
    vmem = pl.BlockSpec(memory_space=pltpu.VMEM)
    dma = pltpu.SemaphoreType.DMA

    def f32(*shape):
        return pltpu.VMEM(shape, F32)

    def b16(*shape):
        return pltpu.VMEM(shape, BF16)

    def row(x):
        return x.reshape(1, COLS)

    array = jax.ShapeDtypeStruct((OWN, COLS), F32)
    line = jax.ShapeDtypeStruct((1, COLS), F32)
    vec = f32(OWN, COLS)
    tables = [pltpu.VMEM((OWN // 16, 256), kind) for kind in (jnp.int32, jnp.int32, F32)]
    parts = pl.pallas_call(
        kernel,
        out_shape=[array] * 4 + [jax.ShapeDtypeStruct((8, COLS), F32)],
        in_specs=[hbm] * 7 + [vmem] * 7,
        out_specs=[hbm] * 4 + [vmem],
        scratch_shapes=[vec] * 5
        + [b16(EXT, HALF), b16(OWN, HALF)]
        + [b16(OWN, EXT), b16(2 * BORDER, OWN), vec] + tables
        + [
            b16(2, OWN, COLS), b16(OWN, 2 * COLS), b16(2 * BORDER, 2 * COLS),
            b16(2, 2 * BORDER, 2 * COLS), b16(3, 2 * BORDER, COLS), b16(2, 2 * BORDER, COLS),
            b16(2, 2 * BORDER, COLS), b16(OWN, COLS), b16(OWN, COLS), vec, vec, vec,
        ]
        + [
            b16(HALF, COLS), b16(HALF, COLS), b16(HALF, COLS), b16(2, OWN - HALF, COLS),
            b16(2, 2, HALF, COLS), b16(2, HALF, COLS), b16(2, OWN, COLS),
            b16(2, 2, HALF, COLS), b16(2, HALF, COLS), b16(2, OWN, COLS),
            b16(HALF, COLS), f32(2, HALF, COLS), b16(HALF, COLS), b16(2, HALF, COLS),
        ]
        + [f32(2, 8, COLS), f32(2, 8, COLS), f32(3, NX * NY, 8, COLS), f32(3, NZ * NC, 8, COLS)]
        + [
            dma((11,)), dma((2, 2)), dma((2, 2)), dma((2, 2)), dma((2, 2, 2)),
            dma((2, 8)), dma((2, 8)), dma((3, 2)), dma((3, 2)),
        ],
        compiler_params=pltpu.CompilerParams(
            collective_id=0, has_side_effects=True, vmem_limit_bytes=60 * 1024 * 1024
        ),
        name="iteration",
    )(
        residual, shadow, direction, old_image, solution, lower_inverse, upper_inverse,
        row(rho_prev), row(alpha_prev), row(omega_prev),
        neighbours, edge_weight, node_shift.reshape(OWN // CHUNK, CHUNK), send_rows,
    )
    steps = 4
    block = pl.BlockSpec((OWN // steps, COLS), lambda i: (i, 0))
    fixed = pl.BlockSpec((1, COLS), lambda i: (0, 0))
    new_solution, new_residual, alpha, omega, rho = pl.pallas_call(
        finish,
        out_shape=[array] * 2 + [line] * 3,
        grid=(steps,),
        in_specs=[block] * 4 + [pl.BlockSpec((8, COLS), lambda i: (0, 0))],
        out_specs=[block] * 2 + [fixed] * 3,
        name="finish",
    )(*parts)
    return new_solution, new_residual, alpha[0], omega[0], rho[0]


def solution(mesh):
    torus = Mesh(
        mesh.devices.reshape(4, 4, 4, 2, mesh.shape["panel"]),
        ("sub_0", "sub_1", "sub_2", "sub_3", "panel"),
    )
    vec = P(SUB, "panel")
    one = P("panel")
    factor = P(SUB, None, "panel")
    in_specs = (
        vec, vec, vec, vec, vec, one, one, one, factor, factor,
        P(None, SUB), P(None, SUB), P(SUB), P(SUB, None, None),
    )
    return jax.shard_map(
        per_device, mesh=torus, in_specs=in_specs, out_specs=(vec, vec, one, one, one), check_vma=False
    )
```

time: 114 us -> 97.8 us (0.86)
  Pallas kernels: 104 us -> 96.8 us
  local copies, waits for them, and re-layouts: 7.16 us -> 0 us
  other arithmetic: 1.27 us -> 0 us
    pallas_call x1 -> x2, Pallas kernels: 104 us -> 96.8 us  [the longest x1 93.2 us: per_device(): pl.pallas_call(kernel, out_shape=[array] * 4 + [jax.ShapeDtypeStruct((8,...]
    unnamed x5 -> x0, local copies, waits for them, and re-layouts: 7.16 us -> none
    another operation x1 -> x0, other arithmetic: 1.27 us -> none  [per_device(): scal = jnp.stack([rho_prev, alpha_prev, omega_prev])]
where the time goes in v2:
time: 97.8 us; the launch traced here: 97.6 us
  Pallas kernels  96.8 us (99%)
    pallas_call x1, Pallas kernels, per_device(): pl.pallas_call(kernel, out_shape=[array] * 4 + [jax.ShapeDtypeStruct((8,...  93.2 us
    pallas_call x1, Pallas kernels, per_device(): pl.pallas_call(finish, out_shape=[array] * 2 + [line] * 3, grid=(steps,),...  3.63 us

profile of v2, /device:TPU:1, one launch (start us, length us, event | category | flops | bytes accessed | tf_op | source)
XLA Modules:
  0.0 97.6 jit_solution(2755507472075763718)
XLA Ops:
  0.6 93.2 %iteration.1 = (f32[1024,128]{1,0:T(8,128)}, f32[1024,128]{1,0:T(8,128)}, f32[1024,128]{1,0:T(8,128)}, f32[1024,128]{1,0:T(8,128)}, f32[8,128]{1,0:T(8,128)}) custom-call(f32[1024,128]{1,0:T(8,128)} %r_hbm.1, f32[1024,128]{1,0:T(8,128)} %s_hbm.1, f32[1024,128]{1,0:T(8,128)} %d_hbm.1, f32[1024,128]{1,0:T(8,128)} %oi_hbm.1, f32[1024,128]{1,0:T(8,128)} %sol_hbm.1, ...), custom_call_target="tpu_custom_call" | custom-call | tf_op jit(solution)/shard_map/iteration/pallas_call | solution.py:493
  93.8 3.6 %finish.1 = (f32[1024,128]{1,0:T(8,128)}, f32[1024,128]{1,0:T(8,128)}, f32[1,128]{1,0:T(1,128)}, f32[1,128]{1,0:T(1,128)}, f32[1,128]{1,0:T(1,128)}) custom-call(f32[1024,128]{1,0:T(8,128)} %get-tuple-element.15.sol, f32[1024,128]{1,0:T(8,128)} %get-tuple-element.16.y, f32[1024,128]{1,0:T(8,128)} %get-tuple-element.17.m, f32[1024,128]{1,0:T(8,128)} %get-tuple-element.18.t, ...), custom_call_target="tpu_custom_call" | custom-call | tf_op jit(solution)/shard_map/finish/pallas_call | solution.py:529

commit v3 on v2

--- a/solution.py
+++ b/solution.py
@@ -37,7 +37,7 @@
     def step(i, carry):
         return body(pl.ds(pl.multiple_of(i * CHUNK, CHUNK), CHUNK), carry)
 
-    return lax.fori_loop(0, OWN // CHUNK, step, init)
+    return lax.fori_loop(0, OWN // CHUNK, step, init, unroll=True)
 
 
 def fold(x):
@@ -62,9 +62,9 @@
     sol_out, y_out_hbm, m_out, t_out, stats,
     r, s, d, oi, sol, low, up,
     w_mat, sel, diag, code_t, base_t, wgt_t,
-    xe, rq, sel_rq, g_rq, sel_u, g_u, g_v, ub, vb, y, v, m,
+    xe, rb, qb, sel_r, g_r, g_q, sel_u, g_u, g_v, ub, vb, y_first, y_second, v, m,
     x1_in, r1_in, v1_in, tail_in, p_in, u_in, y_in, p_out, u_out, y_out, inner, part, x1_c, x2_c,
-    step_own, step_in, ar_a, ar_b,
+    step_own, step_in, middle_sum, red_a0, red_b0, red_a1, red_b1, red_a2, red_b2,
     load_sem, g_send, g_recv, h_send, h_recv, p_send, p_recv, a_send, a_recv,
 ):
     panel = lax.axis_index("panel")
@@ -99,7 +99,6 @@
 
     loads = [
         load(s_hbm, s, 0), load(r_hbm, r, 1), load(d_hbm, d, 2), load(oi_hbm, oi, 3),
-        load(low_hbm.at[0], low, 4), load(up_hbm.at[0, pl.ds(0, OWN)], up, 5), load(sol_hbm, sol, 6),
     ]
 
     barrier = pltpu.get_barrier_semaphore()
@@ -122,28 +121,30 @@
         copy.start()
         sends.append(copy)
 
+    red_a, red_b = (red_a0, red_a1, red_a2), (red_b0, red_b1, red_b2)
+
     def all_of(buf, n, stage, count):
-        every = buf.at[n, pl.ds(0, count)]
+        every = buf.at[pl.ds(0, count)]
         return remote(every, every, a_send.at[n, stage], a_recv.at[n, stage], partner)
 
     def reduce_start(n, rows):
-        mine = ar_a.at[n, ix * NY + iy]
-        mine[...] = jnp.concatenate(rows + [jnp.zeros((8 - len(rows), COLS), F32)], axis=0)
+        mine = red_a[n].at[ix * NY + iy]
+        mine[...] = jnp.concatenate(rows, axis=0)
         for peer in plane:
             remote(mine, mine, a_send.at[n, 0], a_recv.at[n, 0], peer).start()
-        sends.append(all_of(ar_a, n, 0, NX * NY - 1))
+        sends.append(all_of(red_a[n], n, 0, NX * NY - 1))
 
     def reduce_middle(n):
-        all_of(ar_a, n, 0, NX * NY - 1).wait_recv()
-        mine = ar_b.at[n, iz * NC + ic]
-        mine[...] = jnp.sum(ar_a[n], axis=0)
+        all_of(red_a[n], n, 0, NX * NY - 1).wait_recv()
+        mine = red_b[n].at[iz * NC + ic]
+        mine[...] = jnp.sum(red_a[n][...], axis=0)
         for peer in column:
             remote(mine, mine, a_send.at[n, 1], a_recv.at[n, 1], peer).start()
-        sends.append(all_of(ar_b, n, 1, NZ * NC - 1))
+        sends.append(all_of(red_b[n], n, 1, NZ * NC - 1))
 
     def reduce_end(n):
-        all_of(ar_b, n, 1, NZ * NC - 1).wait_recv()
-        return jnp.sum(ar_b[n], axis=0) * (1.0 / (OWN * total))
+        all_of(red_b[n], n, 1, NZ * NC - 1).wait_recv()
+        return jnp.sum(red_b[n][...], axis=0) * (1.0 / (OWN * total))
 
     low_rows, high_rows = pl.ds(0, BORDER), pl.ds(BORDER, BORDER)
 
@@ -169,15 +170,21 @@
 
     loads[0].wait()
     loads[1].wait()
+    loads.extend([
+        load(low_hbm.at[0], low, 4), load(up_hbm.at[0, pl.ds(0, OWN)], up, 5), load(sol_hbm, sol, 6),
+    ])
 
     def opening(at, carry):
         sr, ss = carry
         a, b = s[at, :], r[at, :]
+        rb[at, :] = b.astype(BF16)
         return sr + fold(a * b), ss + fold(a * a)
 
     sr, ss = chunks(opening, (zero, zero))
+    sel_r[0] = dot(sel[...], rb[...]).astype(BF16)
     pl.semaphore_wait(barrier, len(peers))
     reduce_start(0, [jnp.sum(sr, axis=0, keepdims=True), jnp.sum(ss, axis=0, keepdims=True)])
+    ghosts_to_one(sel_r.at[0], g_r, 2)
 
     loads[2].wait()
     loads[3].wait()
@@ -186,23 +193,18 @@
     def combine(at, _):
         q = d[at, :] - omega_before * oi[at, :]
         d[at, :] = q
-        rq[at, 0:COLS] = r[at, :].astype(BF16)
-        rq[at, COLS : 2 * COLS] = q.astype(BF16)
+        qb[at, :] = q.astype(BF16)
         return 0
 
     chunks(combine)
-    sel_rq[...] = dot(sel[...], rq[...]).astype(BF16)
-    ghosts_to_one(sel_rq, g_rq, 0)
+    sel_r[1] = dot(sel[...], qb[...]).astype(BF16)
+    ghosts_to_one(sel_r.at[1], g_q, 0)
 
     def link(src, dst, n, k):
         return remote(src, dst, p_send.at[n, k], p_recv.at[n, k], partner)
 
-    give_r1 = link(rq.at[pl.ds(0, HALF), pl.ds(0, COLS)], r1_in, 0, 7)
+    give_r1 = link(rb.at[pl.ds(0, HALF)], r1_in, 0, 7)
     give_v1 = link(vb.at[pl.ds(0, HALF)], v1_in, 1, 7)
-
-    @pl.when(panel == 1)
-    def _():
-        give_r1.start()
 
     reduce_middle(0)
 
@@ -240,12 +242,23 @@
     def fill(n, k):
         if n == 0:
             lax.fori_loop(k * groups // 4, (k + 1) * groups // 4, build, 0)
+        elif k == 1:
+            step_alpha = step_own[1, 0:1, :]
+
+            def halfway(at, carry):
+                value = r[at, :] - step_alpha * v[at, :]
+                m[at, :] = value
+                sol[at, :] = sol[at, :] + step_alpha * y_first[at, :]
+                return carry + fold(s[at, :] * value)
+
+            middle_sum[...] = chunks(halfway, zero)
 
     q4 = HALF // 2
 
-    def apply(n):
+    def apply(n, y):
         tail = xe.at[n, pl.ds(HALF, OWN - HALF)]
-        give_x1 = link(xe.at[n, pl.ds(0, HALF)], x1_in, n, 0)
+        if n == 0:
+            give_x1 = link(xe.at[n, pl.ds(0, HALF)], x1_in, n, 0)
         give_tail = link(tail, tail_in.at[n], n, 1)
         give_p0 = link(p_out.at[n, 0], p_in.at[n, 0], n, 2)
         give_p1 = link(p_out.at[n, 1], p_in.at[n, 1], n, 3)
@@ -315,16 +328,16 @@
         def _():
             if n == 0:
                 give_x1.start()
+                give_r1.start()
             else:
                 give_step.start()
 
             def extended(c, own_tail, step):
                 x2_c[c, 0 : OWN - HALF, :] = own_tail
-                g_r = g_rq[c, :, 0:COLS].astype(F32)
                 if n == 0:
-                    value = g_r + step * g_rq[c, :, COLS : 2 * COLS].astype(F32)
+                    value = g_r[c].astype(F32) + step * g_q[c].astype(F32)
                 else:
-                    value = g_r - step * g_v[c].astype(F32)
+                    value = g_r[c].astype(F32) - step * g_v[c].astype(F32)
                 x2_c[c, OWN - HALF : HALF, :] = value.astype(BF16)
                 part[c, 0:q4, :] = dot(low[HALF : HALF + q4, 0:q4], x2_c[c, 0:q4, :])
                 part[c, q4:HALF, :] = dot(low[HALF + q4 : EXT, :], x2_c[c])
@@ -335,10 +348,14 @@
                     at = slice(h * (OWN // 2), (h + 1) * (OWN // 2))
                     put(at, dot(up[at, :], inner[...]))
 
-            received = g_rq if n == 0 else g_v
+            received = g_q if n == 0 else g_v
             fill(n, 0)
+            if n == 0:
+                ghosts_at_one(g_r, 2, 1)
             ghosts_at_one(received, n, 1)
             extended(1, xe[n, HALF:OWN, :], step_own[n, 0:1, :])
+            if n == 0:
+                ghosts_at_one(g_r, 2, 0)
             ghosts_at_one(received, n, 0)
             give_step.wait_recv()
             give_tail.wait_recv()
@@ -375,7 +392,7 @@
                 give_step.wait_send()
                 give_v1.wait_send()
 
-    def operate(n, use):
+    def operate(n, y, use):
         sel_u[n, 0:BORDER, :] = dot(sel[0:BORDER, :], ub[...]).astype(BF16)
         send(sel_u.at[n, low_rows], g_u.at[n, high_rows], g_send.at[n, 0], g_recv.at[n, 0], below)
         sel_u[n, BORDER:, :] = dot(sel[BORDER:, :], ub[...]).astype(BF16)
@@ -403,7 +420,7 @@
     chunks(direct)
     loads[4].wait()
     loads[5].wait()
-    apply(0)
+    apply(0, y_first)
 
     sums = []
 
@@ -412,7 +429,7 @@
         vb[at, :] = value.astype(BF16)
         sums.append((whole(s[at, :] * value), whole(value * value)))
 
-    operate(0, image)
+    operate(0, y_first, image)
     reduce_start(1, [sums[0][i] + sums[1][i] for i in range(2)])
 
     @pl.when(panel == 1)
@@ -430,27 +447,23 @@
     )
     step_own[1] = jnp.broadcast_to(step_alpha, (8, COLS))
 
-    def halfway(at, carry):
-        value = r[at, :] - step_alpha * v[at, :]
-        m[at, :] = value
-        xe[1, at, :] = value.astype(BF16)
-        sol[at, :] = sol[at, :] + step_alpha * y[at, :]
-        return carry + fold(s[at, :] * value)
-
-    shadow_middle = chunks(halfway, zero)
-    store = [load(sol, sol_out, 7), load(m, m_out, 8)]
-    apply(1)
-    store.append(load(y, y_out_hbm, 9))
+    def middle(at, _):
+        xe[1, at, :] = (r[at, :] - step_alpha * v[at, :]).astype(BF16)
+        return 0
+
+    chunks(middle)
+    apply(1, y_second)
+    store = [load(sol, sol_out, 7), load(m, m_out, 8), load(y_second, y_out_hbm, 9)]
     sums = []
 
     def test(at, value):
         v[at, :] = value
         sums.append((whole(value * m[at, :]), whole(value * value), whole(s[at, :] * value)))
 
-    operate(1, test)
+    operate(1, y_second, test)
     store.append(load(v, t_out, 10))
     tm, tt, st = (sums[0][i] + sums[1][i] for i in range(3))
-    reduce_start(2, [tm, tt, whole(shadow_middle), st])
+    reduce_start(2, [tm, tt, whole(middle_sum[...]), st])
     reduce_middle(2)
     mean = reduce_end(2)
     stats[...] = jnp.concatenate([mean[0:4, :], step_alpha, jnp.zeros((3, COLS), F32)], axis=0)
@@ -499,9 +512,9 @@
         + [b16(EXT, HALF), b16(OWN, HALF)]
         + [b16(OWN, EXT), b16(2 * BORDER, OWN), vec] + tables
         + [
-            b16(2, OWN, COLS), b16(OWN, 2 * COLS), b16(2 * BORDER, 2 * COLS),
-            b16(2, 2 * BORDER, 2 * COLS), b16(3, 2 * BORDER, COLS), b16(2, 2 * BORDER, COLS),
-            b16(2, 2 * BORDER, COLS), b16(OWN, COLS), b16(OWN, COLS), vec, vec, vec,
+            b16(2, OWN, COLS), b16(OWN, COLS), b16(OWN, COLS), b16(2, 2 * BORDER, COLS),
+            b16(2, 2 * BORDER, COLS), b16(2, 2 * BORDER, COLS), b16(3, 2 * BORDER, COLS), b16(2, 2 * BORDER, COLS),
+            b16(2, 2 * BORDER, COLS), b16(OWN, COLS), b16(OWN, COLS), vec, vec, vec, vec,
         ]
         + [
             b16(HALF, COLS), b16(HALF, COLS), b16(HALF, COLS), b16(2, OWN - HALF, COLS),
@@ -509,9 +522,10 @@
             b16(2, 2, HALF, COLS), b16(2, HALF, COLS), b16(2, OWN, COLS),
             b16(HALF, COLS), f32(2, HALF, COLS), b16(HALF, COLS), b16(2, HALF, COLS),
         ]
-        + [f32(2, 8, COLS), f32(2, 8, COLS), f32(3, NX * NY, 8, COLS), f32(3, NZ * NC, 8, COLS)]
+        + [f32(2, 8, COLS), f32(2, 8, COLS), f32(8, COLS)]
+        + [f32(k, rows, COLS) for rows in (2, 2, 4) for k in (NX * NY, NZ * NC)]
         + [
-            dma((11,)), dma((2, 2)), dma((2, 2)), dma((2, 2)), dma((2, 2, 2)),
+            dma((11,)), dma((2, 2)), dma((2, 2)), dma((3, 2)), dma((3, 2, 2)),
             dma((2, 8)), dma((2, 8)), dma((3, 2)), dma((3, 2)),
         ],
         compiler_params=pltpu.CompilerParams(
@@ -523,7 +537,7 @@
         row(rho_prev), row(alpha_prev), row(omega_prev),
         neighbours, edge_weight, node_shift.reshape(OWN // CHUNK, CHUNK), send_rows,
     )
-    steps = 4
+    steps = 1
     block = pl.BlockSpec((OWN // steps, COLS), lambda i: (i, 0))
     fixed = pl.BlockSpec((1, COLS), lambda i: (0, 0))
     new_solution, new_residual, alpha, omega, rho = pl.pallas_call(

time: 97.8 us -> 94.9 us (0.970)
  Pallas kernels: 96.8 us -> 94.1 us
    pallas_call x1, Pallas kernels: 93.2 us -> 91.5 us  [per_device(): pl.pallas_call(kernel, out_shape=[array] * 4 + [jax.ShapeDtypeStruct((8,...]
    pallas_call x1, Pallas kernels: 3.63 us -> 2.55 us  [per_device(): pl.pallas_call(finish, out_shape=[array] * 2 + [line] * 3, grid=(steps,),...]
where the time goes in v3:
time: 94.9 us; the launch traced here: 94.7 us
  Pallas kernels  94.1 us (99%)
    pallas_call x1, Pallas kernels, per_device(): pl.pallas_call(kernel, out_shape=[array] * 4 + [jax.ShapeDtypeStruct((8,...  91.5 us
    pallas_call x1, Pallas kernels, per_device(): pl.pallas_call(finish, out_shape=[array] * 2 + [line] * 3, grid=(steps,),...  2.55 us

profile of v3, /device:TPU:1, one launch (start us, length us, event | category | flops | bytes accessed | tf_op | source)
XLA Modules:
  0.0 94.7 jit_solution(5844250833257406323)
XLA Ops:
  0.6 91.5 %iteration.1 = (f32[1024,128]{1,0:T(8,128)}, f32[1024,128]{1,0:T(8,128)}, f32[1024,128]{1,0:T(8,128)}, f32[1024,128]{1,0:T(8,128)}, f32[8,128]{1,0:T(8,128)}) custom-call(f32[1024,128]{1,0:T(8,128)} %r_hbm.1, f32[1024,128]{1,0:T(8,128)} %s_hbm.1, f32[1024,128]{1,0:T(8,128)} %d_hbm.1, f32[1024,128]{1,0:T(8,128)} %oi_hbm.1, f32[1024,128]{1,0:T(8,128)} %sol_hbm.1, ...), custom_call_target="tpu_custom_call" | custom-call | tf_op jit(solution)/shard_map/iteration/pallas_call | solution.py:506
  92.2 2.6 %finish.1 = (f32[1024,128]{1,0:T(8,128)}, f32[1024,128]{1,0:T(8,128)}, f32[1,128]{1,0:T(1,128)}, f32[1,128]{1,0:T(1,128)}, f32[1,128]{1,0:T(1,128)}) custom-call(f32[1024,128]{1,0:T(8,128)} %get-tuple-element.15.sol, f32[1024,128]{1,0:T(8,128)} %get-tuple-element.16.y, f32[1024,128]{1,0:T(8,128)} %get-tuple-element.17.m, f32[1024,128]{1,0:T(8,128)} %get-tuple-element.18.t, ...), custom_call_target="tpu_custom_call" | custom-call | tf_op jit(solution)/shard_map/finish/pallas_call | solution.py:543

commit v4 on v3

--- a/solution.py
+++ b/solution.py
@@ -82,6 +82,8 @@
     total = NX * NY * NZ * NC
     above = coords((flat + 1) % total)
     below = coords((flat + total - 1) % total)
+    far_peer = coords((flat + total + 2 * ic - 1) % total)
+    near_peer = coords((flat + total + 1 - 2 * ic) % total)
     above_one = {**above, "panel": 1}
     below_one = {**below, "panel": 1}
     partner = {"panel": 1 - panel}
@@ -198,7 +200,6 @@
 
     chunks(combine)
     sel_r[1] = dot(sel[...], qb[...]).astype(BF16)
-    ghosts_to_one(sel_r.at[1], g_q, 0)
 
     def link(src, dst, n, k):
         return remote(src, dst, p_send.at[n, k], p_recv.at[n, k], partner)
@@ -207,6 +208,7 @@
     give_v1 = link(vb.at[pl.ds(0, HALF)], v1_in, 1, 7)
 
     reduce_middle(0)
+    ghosts_to_one(sel_r.at[1], g_q, 0)
 
     valid = nbr[...] < EXT
     present = jnp.sum(jnp.where(valid, ew[...], 0.0), axis=0, keepdims=True)
@@ -393,17 +395,24 @@
                 give_v1.wait_send()
 
     def operate(n, y, use):
-        sel_u[n, 0:BORDER, :] = dot(sel[0:BORDER, :], ub[...]).astype(BF16)
-        send(sel_u.at[n, low_rows], g_u.at[n, high_rows], g_send.at[n, 0], g_recv.at[n, 0], below)
-        sel_u[n, BORDER:, :] = dot(sel[BORDER:, :], ub[...]).astype(BF16)
-        send(sel_u.at[n, high_rows], g_u.at[n, low_rows], g_send.at[n, 1], g_recv.at[n, 1], above)
-        copies = sends[-2:]
+        for k, peer in ((ic, far_peer), (1 - ic, near_peer)):
+            mine = pl.ds(pl.multiple_of(k * BORDER, CHUNK), BORDER)
+            theirs = pl.ds(pl.multiple_of((1 - k) * BORDER, CHUNK), BORDER)
+            sel_u[n, mine, :] = dot(sel[mine, :], ub[...]).astype(BF16)
+            send(sel_u.at[n, mine], g_u.at[n, theirs], g_send.at[n, k], g_recv.at[n, k], peer)
         v[...] = diag[...] * y[...] - dot(w_mat[:, 0:OWN], ub[...])
-        for copy in copies:
-            copy.wait_recv()
+
+        def arrived(k):
+            theirs = pl.ds(pl.multiple_of((1 - k) * BORDER, CHUNK), BORDER)
+            remote(g_u.at[n, theirs], g_u.at[n, theirs], g_send.at[n, k], g_recv.at[n, k], partner).wait_recv()
+            return g_u[n, theirs, :], pl.ds(pl.multiple_of(OWN + (1 - k) * BORDER, CHUNK), BORDER)
+
+        rows, cols = arrived(ic)
+        v[...] = v[...] - dot(w_mat[:, cols], rows)
+        rows, cols = arrived(1 - ic)
         for h in range(2):
             at = slice(h * (OWN // 2), (h + 1) * (OWN // 2))
-            use(at, v[at, :] - dot(w_mat[at, OWN:EXT], g_u[n]))
+            use(at, v[at, :] - dot(w_mat[at, cols], rows))
 
     def whole(x):
         return jnp.sum(x, axis=0, keepdims=True)
@@ -437,9 +446,9 @@
         give_v1.start()
 
     sel_u[2] = dot(sel[...], vb[...]).astype(BF16)
-    ghosts_to_one(sel_u.at[2], g_v, 1)
     loads[6].wait()
     reduce_middle(1)
+    ghosts_to_one(sel_u.at[2], g_v, 1)
     mean = reduce_end(1)
     denominator, image_square = mean[0:1, :], mean[1:2, :]
     step_alpha = rho_now / jnp.maximum(

time: 94.9 us -> 89.2 us (0.940)
  Pallas kernels: 94.1 us -> 88.4 us
    pallas_call x1, Pallas kernels: 91.5 us -> 85.8 us  [per_device(): pl.pallas_call(kernel, out_shape=[array] * 4 + [jax.ShapeDtypeStruct((8,...]
where the time goes in v4:
time: 89.2 us; the launch traced here: 89 us
  Pallas kernels  88.4 us (99%)
    pallas_call x1, Pallas kernels, per_device(): pl.pallas_call(kernel, out_shape=[array] * 4 + [jax.ShapeDtypeStruct((8,...  85.8 us
    pallas_call x1, Pallas kernels, per_device(): pl.pallas_call(finish, out_shape=[array] * 2 + [line] * 3, grid=(steps,),...  2.55 us

profile of v4, /device:TPU:1, one launch (start us, length us, event | category | flops | bytes accessed | tf_op | source)
XLA Modules:
  0.0 89.0 jit_solution(13689612799655099241)
XLA Ops:
  0.6 85.8 %iteration.1 = (f32[1024,128]{1,0:T(8,128)}, f32[1024,128]{1,0:T(8,128)}, f32[1024,128]{1,0:T(8,128)}, f32[1024,128]{1,0:T(8,128)}, f32[8,128]{1,0:T(8,128)}) custom-call(f32[1024,128]{1,0:T(8,128)} %r_hbm.1, f32[1024,128]{1,0:T(8,128)} %s_hbm.1, f32[1024,128]{1,0:T(8,128)} %d_hbm.1, f32[1024,128]{1,0:T(8,128)} %oi_hbm.1, f32[1024,128]{1,0:T(8,128)} %sol_hbm.1, ...), custom_call_target="tpu_custom_call" | custom-call | tf_op jit(solution)/shard_map/iteration/pallas_call | solution.py:515
  86.4 2.6 %finish.1 = (f32[1024,128]{1,0:T(8,128)}, f32[1024,128]{1,0:T(8,128)}, f32[1,128]{1,0:T(1,128)}, f32[1,128]{1,0:T(1,128)}, f32[1,128]{1,0:T(1,128)}) custom-call(f32[1024,128]{1,0:T(8,128)} %get-tuple-element.15.sol, f32[1024,128]{1,0:T(8,128)} %get-tuple-element.16.y, f32[1024,128]{1,0:T(8,128)} %get-tuple-element.17.m, f32[1024,128]{1,0:T(8,128)} %get-tuple-element.18.t, ...), custom_call_target="tpu_custom_call" | custom-call | tf_op jit(solution)/shard_map/finish/pallas_call | solution.py:552

commit v5 on v4

--- a/solution.py
+++ b/solution.py
@@ -239,11 +239,13 @@
             w_mat[at, a * COLS : (a + 1) * COLS] = found[a * 16 : (a + 1) * 16, :]
         return 0
 
-    groups = OWN // 16
+    groups, part_size = OWN // 16, 13
+    early = groups - 4 * part_size
+    lax.fori_loop(0, early, build, 0)
 
     def fill(n, k):
         if n == 0:
-            lax.fori_loop(k * groups // 4, (k + 1) * groups // 4, build, 0)
+            lax.fori_loop(early + k * part_size, early + (k + 1) * part_size, build, 0)
         elif k == 1:
             step_alpha = step_own[1, 0:1, :]
 

time: 89.2 us -> 90.5 us (1.015)
  Pallas kernels: 88.4 us -> 89.6 us
    pallas_call x1, Pallas kernels: 85.8 us -> 87 us  [per_device(): pl.pallas_call(kernel, out_shape=[array] * 4 + [jax.ShapeDtypeStruct((8,...]
where the time goes in v5:
time: 90.5 us; the launch traced here: 90.2 us
  Pallas kernels  89.6 us (99%)
    pallas_call x1, Pallas kernels, per_device(): pl.pallas_call(kernel, out_shape=[array] * 4 + [jax.ShapeDtypeStruct((8,...  87 us
    pallas_call x1, Pallas kernels, per_device(): pl.pallas_call(finish, out_shape=[array] * 2 + [line] * 3, grid=(steps,),...  2.55 us

profile of v5, /device:TPU:1, one launch (start us, length us, event | category | flops | bytes accessed | tf_op | source)
XLA Modules:
  0.0 90.2 jit_solution(5402240376015584145)
XLA Ops:
  0.6 87.0 %iteration.1 = (f32[1024,128]{1,0:T(8,128)}, f32[1024,128]{1,0:T(8,128)}, f32[1024,128]{1,0:T(8,128)}, f32[1024,128]{1,0:T(8,128)}, f32[8,128]{1,0:T(8,128)}) custom-call(f32[1024,128]{1,0:T(8,128)} %r_hbm.1, f32[1024,128]{1,0:T(8,128)} %s_hbm.1, f32[1024,128]{1,0:T(8,128)} %d_hbm.1, f32[1024,128]{1,0:T(8,128)} %oi_hbm.1, f32[1024,128]{1,0:T(8,128)} %sol_hbm.1, ...), custom_call_target="tpu_custom_call" | custom-call | tf_op jit(solution)/shard_map/iteration/pallas_call | solution.py:517
  87.7 2.6 %finish.1 = (f32[1024,128]{1,0:T(8,128)}, f32[1024,128]{1,0:T(8,128)}, f32[1,128]{1,0:T(1,128)}, f32[1,128]{1,0:T(1,128)}, f32[1,128]{1,0:T(1,128)}) custom-call(f32[1024,128]{1,0:T(8,128)} %get-tuple-element.15.sol, f32[1024,128]{1,0:T(8,128)} %get-tuple-element.16.y, f32[1024,128]{1,0:T(8,128)} %get-tuple-element.17.m, f32[1024,128]{1,0:T(8,128)} %get-tuple-element.18.t, ...), custom_call_target="tpu_custom_call" | custom-call | tf_op jit(solution)/shard_map/finish/pallas_call | solution.py:554
